TPU v7x, 32 devices: a whole 2x2x4 slice. The times are simulated.
32 devices in a mesh: round: 2 (over x), brick: 16 (over z, y, core).
Axes of the slice: x: 2, y: 2, z: 4, core: 2. Of those that a mesh axis runs over, the one named last changes fastest.
Arguments:
- image: bfloat16 [2, 128, 4, 32, 8, 128], P('round', 'brick'), may hold values from -60 to 60
- shifts: int32 [2, 128], P('round', 'brick'), may hold values from -24 to 24, as said below
- fractions: float32 [2, 128], P('round', 'brick'), may hold values from 0 to 1
- valid: int32 [128], replicated, may hold values from 0 to 1, as said below
Outputs:
- spots: bfloat16 [2, 2, 64, 4, 32, 8, 128], P(None, 'round', 'brick')
Inputs may be any that keep to these rules, and one draw needn't show every extreme that they name: `shifts`: in every round, the last brick of each aligned block of 8 bricks has a shift between minus 24 and minus half of 24 (rounded down), and the first brick of each such block a shift between half of 24 (rounded down) and 24. `valid`: the first and the last brick of each aligned block of 8 bricks hold tissue.
All inputs are finite; a program needn't handle non-finite values.
Results may differ from a plain program's by a relative error of at most 0.0055.
Values may be sent and summed in bfloat16 or wider, within the bound.
No kernel may reach another device: no remote copies, remote signals or barrier semaphores. Data moves between devices by JAX's collectives and lax.ppermute only.
A program may use at most 128 MiB of HBM per device.

v0:
```python
import functools

import jax
import jax.numpy as jnp
import numpy as np
from jax import lax
from jax.experimental import pallas as pl
from jax.experimental.pallas import tpu as pltpu
from jax.sharding import PartitionSpec as P

sigma_spot = 1.5


BF = jnp.bfloat16
F32 = jnp.float32
VMEM = pl.BlockSpec(memory_space=pltpu.VMEM)
SMEM = pl.BlockSpec(memory_space=pltpu.SMEM)
HBM = pl.BlockSpec(memory_space=pltpu.HBM)
CHUNKS = 4
HALVES = 2
PARAMS = pltpu.CompilerParams(vmem_limit_bytes=24 * 2**20)


def kernel_tables(count):
    index = np.arange(count, dtype=np.float64)
    offset = index[:, None] - index[None, :]
    smooth = np.exp(-offset * offset / (2.0 * sigma_spot * sigma_spot)) / (
        2.5066282746310002 * sigma_spot
    )
    smooth = np.where(np.abs(offset) < 4.0 * sigma_spot, smooth, 0.0)
    curve = (offset * offset / sigma_spot**4 - 1.0 / sigma_spot**2) * smooth
    return smooth, curve


def plane_tables(depth, height):
    gauss_z, curve_z = kernel_tables(depth)
    gauss_y, curve_y = kernel_tables(height)
    factor = -(sigma_spot * sigma_spot)
    with_bent = np.kron(gauss_z, gauss_y)
    with_smooth = np.kron(gauss_z, curve_y) + np.kron(curve_z, gauss_y)
    table = (factor * np.concatenate([with_bent, with_smooth], axis=0)).astype(np.float32)
    high = table.astype(BF)
    low = (table - high.astype(np.float32)).astype(BF)
    return np.concatenate([high, low], axis=0)


def line_tables(width):
    gauss_x, curve_x = kernel_tables(width)
    return np.stack([np.tile(t.T, (2, 1)) for t in (curve_x, gauss_x)]).astype(np.float32)


def lanes_of(shape):
    return lax.broadcasted_iota(jnp.int32, shape, len(shape) - 1)


def pack(valid_ref, img_ref, is_tail):
    bricks, channels, plane, width = img_ref.shape
    slot = width // channels
    first = lax.axis_index("brick") * bricks
    lane = lanes_of((plane, width))
    brick = jnp.where(is_tail, bricks - 1, 0)
    at = jnp.where(is_tail, width - slot, 0)
    row = jnp.zeros((plane, width), F32)
    for c in range(channels):
        data = img_ref[brick, c].astype(F32)
        moved = pltpu.roll(data, lax.rem(c * slot + width - at, width), 1)
        row = jnp.where(lane // slot == c, moved, row)
    return (row * valid_ref[first + brick].astype(F32)).astype(BF)


def swaps_of(count):
    both = lambda couples: [link for a, b in couples for link in ((a, b), (b, a))]
    even = both([(i, i + 1) for i in range(0, count - 1, 2)])
    if count % 4 or count < 8:
        return [even, both([(i, i + 1) for i in range(1, count - 1, 2)])]
    second = both([(i + 1, i + 2) for i in range(0, count, 4)] + [(i, i + 3) for i in range(0, count, 4)])
    third = both([(i, i + 1) for i in range(3, count - 1, 4)] + [(i, i + 1) for i in range(5, count - 4, 4)])
    for a, b, c in ((0, 1, 2), (count - 3, count - 2, count - 1)):
        third += [(a, b), (b, c), (c, a)]
    return [even, second, third]


class Filter:
    def __init__(self, shift_ref, frac_ref, valid_ref, img_ref, plane_ref=None, line_ref=None, halo=()):
        self.shift, self.frac, self.valid = shift_ref, frac_ref, valid_ref
        self.img, self.plane, self.line, self.halo = img_ref, plane_ref, line_ref, halo

    def valid_of(self, b):
        return self.valid[lax.axis_index("brick") * self.shift.shape[1] + b].astype(F32)

    def field(self, b, at, turned):
        bricks = self.shift.shape[1]
        _, channels, plane, width = self.img.shape
        slot = width // channels
        tiles = (plane // 8, 8, width)
        lane = lanes_of((8, width))
        s = self.shift[0, b]
        f = self.frac[0, b]
        right = s >= 0
        nb = jnp.where(right, b - 1, b + 1)
        nb_in = jnp.clip(nb, 0, bricks - 1)
        first = lax.axis_index("brick") * bricks
        own_valid = self.valid_of(b)
        nb_valid = self.valid_of(nb_in)
        if self.halo:
            there_is = jnp.logical_and(first + nb >= 0, first + nb < self.valid.shape[0])
            nb_valid = jnp.where(nb == nb_in, nb_valid, there_is.astype(F32))
            index = lax.axis_index("brick")
            in_first = (nb < 0) == (lax.rem(index, 2) == 1)
            second, third = self.halo[1], self.halo[-1]
            in_second = lax.rem(index, 4) % 3 != 0
            halo = jnp.where(in_second, second[...], third[...])
            halo = jnp.where(in_first, self.halo[0][...], halo).astype(F32).reshape(tiles)
            start = jnp.where(nb < 0, width - slot, 0)
        low0, high0 = jnp.where(right, 0, -s), jnp.where(right, width - s, width)
        low1, high1 = jnp.where(right, 0, -s - 1), jnp.where(right, width - s - 1, width)
        own0 = (lane >= low0) & (lane < high0)
        own1 = (lane >= low1) & (lane < high1)
        gain0 = (1.0 - f) * jnp.where(own0, own_valid, nb_valid)
        gain1 = f * jnp.where(own1, own_valid, nb_valid)
        own0, own1 = (jnp.broadcast_to(m, tiles) for m in (own0, own1))
        parts = []
        for c in range(channels):
            own = self.img[at(b), c].astype(F32).reshape(tiles)
            other = self.img[at(nb_in), c].astype(F32).reshape(tiles)
            if self.halo:
                moved = pltpu.roll(halo, lax.rem(start + (width - c * slot), width), 2)
                other = jnp.where(nb == nb_in, other, moved)
            here = jnp.where(own0, own, other) * gain0
            there = jnp.where(own1, own, other) * gain1
            value = here + pltpu.roll(there, 1, 2)
            if turned:
                value = pltpu.roll(value, self.turn_of(b), 2)
            parts.append(value.reshape(plane, width).astype(BF))
        return parts

    def turn_of(self, b):
        s = self.shift[0, b]
        return jnp.where(s < 0, s + self.img.shape[-1], s)

    def apply(self, parts, turn, put, totals, weight):
        plane, width = parts[0].shape
        field = jnp.concatenate(parts, axis=1)
        dot = functools.partial(jnp.dot, preferred_element_type=F32)
        half = 2 * plane
        mixed = dot(self.plane[:half], field) + dot(self.plane[half:], field)
        line = jnp.concatenate([self.line[k, pl.ds(turn, width), :] for k in range(2)], axis=0)
        line_high = line.astype(BF)
        line_low = (line - line_high.astype(F32)).astype(BF)
        lines = jnp.concatenate([line_high, line_low], axis=1)
        added = []
        for c, total in enumerate(totals):
            wide = jnp.concatenate(
                [mixed[k * plane : (k + 1) * plane, c * width : (c + 1) * width] for k in range(2)],
                axis=1,
            )
            both = dot(wide.astype(BF), lines)
            result = (both[:, :width] + both[:, width:]).astype(BF)
            put(c, result)
            size = jnp.abs(result.astype(F32)).reshape(plane // 8, 8, width)
            added.append(total + jnp.sum(size, axis=0) * weight)
        return added

    def __call__(self, b, put, totals):
        parts = self.field(b, lambda n: n, False)
        return self.apply(parts, self.turn_of(b), put, totals, self.valid_of(b))


def put_in(refs, n):
    def put(c, value):
        rows = value.shape[0] // len(refs)
        for k, ref in enumerate(refs):
            ref[n, c] = value[k * rows : (k + 1) * rows]

    return put


def load_kernel(picks, shift_hbm, frac_hbm, valid_hbm, img_ref, *refs):
    part_refs, refs = refs[: len(picks)], refs[len(picks) :]
    shift_ref, frac_ref, valid_ref, near_ref, near_sem, small_sem = refs
    bricks = img_ref.shape[0]
    rank = lax.axis_index("round")
    pairs = [(shift_hbm, shift_ref), (frac_hbm, frac_ref), (valid_hbm, valid_ref)]
    copies = [pltpu.make_async_copy(a, b, small_sem.at[n]) for n, (a, b) in enumerate(pairs)]
    bases = [pick(rank) - 1 for pick in picks]
    for k, base in enumerate(bases):
        for n in range(3):
            b = jnp.clip(base + n, 0, bricks - 1)
            copies.append(pltpu.make_async_copy(img_ref.at[b], near_ref.at[3 * k + n], near_sem.at[3 * k + n]))
    for copy in copies:
        copy.start()
    for copy in copies:
        copy.wait()
    one = Filter(shift_ref, frac_ref, valid_ref, near_ref)
    for k, (base, part_ref) in enumerate(zip(bases, part_refs, strict=True)):
        parts = one.field(base + 1, lambda n, k=k, base=base: n - base + 3 * k, True)
        for c, part in enumerate(parts):
            part_ref[0, c] = part


def pack_kernel(valid_ref, img_ref, swap0_ref, swap1_ref):
    even = lax.rem(lax.axis_index("brick"), 2) == 0
    swap0_ref[...] = pack(valid_ref, img_ref, even)
    swap1_ref[...] = pack(valid_ref, img_ref, jnp.logical_not(even))


def filter_kernel(groups, first, edge, shift_ref, frac_ref, valid_ref, img_ref, plane_ref, line_ref, *refs):
    sums_ref = None
    halo, refs = refs[:edge], refs[edge:]
    if not first:
        sums_ref, refs = refs[0], refs[1:]
    *out_refs, stat_ref = refs
    _, channels, _, width = img_ref.shape
    rank = lax.axis_index("round")
    one = Filter(shift_ref, frac_ref, valid_ref, img_ref, plane_ref, line_ref, halo)
    totals = [jnp.zeros((8, width), F32) if first else sums_ref[c] for c in range(channels)]
    for picks, halves in groups:
        refs, out_refs = out_refs[:halves], out_refs[halves:]
        for n, pick in enumerate(picks):
            totals = one(pick(rank), put_in(refs, n), totals)
    for c in range(channels):
        stat_ref[c] = totals[c]


def close_kernel(pick, shift_ref, frac_ref, valid_ref, plane_ref, line_ref, sums_ref, *refs):
    *refs, stat_ref = refs
    peers = len(refs) // 2
    part_refs, out_refs = refs[:peers], refs[peers:]
    channels, _, width = sums_ref.shape
    rank = lax.axis_index("round")
    one = Filter(shift_ref, frac_ref, valid_ref, None, plane_ref, line_ref)
    found = [sums_ref[c] for c in range(channels)]
    for part_ref, out_ref in zip(part_refs, out_refs, strict=True):
        parts = [part_ref[0, c] for c in range(channels)]
        totals = [jnp.zeros((8, width), F32) for _ in range(channels)]
        found += one.apply(parts, 0, put_in([out_ref], 0), totals, one.valid_of(pick(rank)))
    packed = jnp.zeros(stat_ref.shape[1:], F32)
    for n, total in enumerate(found):
        packed = jnp.where(lanes_of(packed.shape) == n, jnp.sum(total), packed)
    stat_ref[...] = jnp.broadcast_to(packed, stat_ref.shape)


def norm_kernel(rounds, tasks, out_ref, inverse_ref, data_refs, buf_refs, kept_ref, sem):
    _, channels, plane, width = out_ref.shape[2:]
    step = plane // CHUNKS
    tiles = (step // 8, 8, width)
    copies = []
    stored, kept = 0, 0
    for j, n, sources, keep in tasks:

        def ratio(d, c):
            g, m, base = sources[d]
            data = data_refs[g][m, c, n * step - base : (n + 1) * step - base]
            return data.astype(F32).reshape(tiles) * inverse_ref[d, c]

        energy = jnp.zeros(tiles, F32)
        for d in range(rounds):
            for c in range(channels):
                part = ratio(d, c)
                energy = energy + part * part
        factor = lax.rsqrt(energy * (1.0 / (rounds * channels)) + 1.0)
        to_ref, m = (kept_ref, kept) if keep else (buf_refs, stored)
        for d in range(rounds):
            for c in range(channels):
                to_ref[m, d, c] = (ratio(d, c) * factor).reshape(step, width).astype(BF)
        if keep:
            kept += 1
        else:
            copies += store(rounds, j, n, buf_refs.at[m], out_ref, sem.at[m])
            stored += 1
    return copies


def store(rounds, j, n, from_ref, out_ref, sem):
    quota, _, plane, _ = out_ref.shape[2:]
    rank = lax.axis_index("round")
    pos = jnp.where(rank == 0, quota - 1 - j, j)
    step = plane // CHUNKS
    copies = []
    for d in range(rounds):
        slot = lax.rem(rank + rounds - d, rounds)
        to_ref = out_ref.at[slot, 0, pos, :, pl.ds(n * step, step)]
        copy = pltpu.make_async_copy(from_ref.at[d], to_ref, sem.at[d])
        copy.start()
        copies.append(copy)
    return copies


def norm1_kernel(rounds, shared, tasks, valid_ref, stat_ref, *refs):
    *data_refs, out_ref, inverse_ref, kept_ref, buf_ref, sem = refs
    _, channels, plane, width = out_ref.shape[2:]
    rank = lax.axis_index("round")
    count = jnp.maximum(jnp.sum(valid_ref[...]).astype(F32), 1.0)
    each = stat_ref.shape[0] // rounds
    for d in range(rounds):
        slot = lax.rem(rank + rounds - d, rounds)
        total = jnp.zeros(stat_ref.shape[1:], F32)
        for e in range(rounds if shared else 1):
            part = jnp.sum(stat_ref[pl.ds(lax.rem(slot + e, rounds) * each, each)], axis=0)
            total = total + (pltpu.roll(part, width - e * channels, 1) if e else part)
        scale = total / (count * (plane * width)) + 1e-06
        for c in range(channels):
            inverse_ref[d, c] = jnp.broadcast_to((1.0 / scale)[:, c : c + 1], (8, width))
    for copy in norm_kernel(rounds, tasks, out_ref, inverse_ref, data_refs, buf_ref, kept_ref, sem):
        copy.wait()


def norm2_kernel(rounds, tasks, carried, result_ref, inverse_ref, kept_ref, *refs):
    *data_refs, out_ref, buf_ref, sem, kept_sem = refs
    copies = []
    for m, (j, n) in enumerate(carried):
        copies += store(rounds, j, n, kept_ref.at[m], out_ref, kept_sem.at[m])
    copies += norm_kernel(rounds, tasks, out_ref, inverse_ref, data_refs, buf_ref, None, sem)
    for copy in copies:
        copy.wait()


def in_vmem(x):
    return pltpu.with_memory_space_constraint(x, pltpu.VMEM)


def in_smem(x):
    return pltpu.with_memory_space_constraint(x, pltpu.SMEM)


def in_hbm(x):
    return pltpu.with_memory_space_constraint(x, pltpu.HBM)


def body(image, shifts, fractions, valid):
    _, bricks, channels, depth, height, width = image.shape
    plane = depth * height
    rounds = lax.axis_size("round")
    count = lax.axis_size("brick")
    quota = bricks // rounds
    img = image.reshape(bricks, channels, plane, width)
    plane_table = jnp.asarray(plane_tables(depth, height))
    line_table = jnp.asarray(line_tables(width))

    def out(shape, dtype):
        return pltpu.VMEM(shape, dtype)

    def pick_for(d, j):
        def pick(rank):
            target = lax.rem(rank + d, rounds)
            return target * quota + jnp.where(target == 0, quota - 1 - j, j)

        return pick

    peers = range(1, rounds)
    early = [0] if quota > 1 else []
    inner = list(range(1, quota - 1))
    sum_shape = out((channels, 8, width), F32)
    firsts = [pick_for(d, 0) for d in peers] if early else []
    sources = [shifts, fractions, valid]

    *parts, shift_s, frac_s, valid_s = pl.pallas_call(
        functools.partial(load_kernel, firsts),
        in_specs=[HBM] * 4,
        out_specs=[VMEM] * len(firsts) + [SMEM] * 3,
        out_shape=[out((1, channels, plane, width), BF)] * len(firsts)
        + [pltpu.SMEM(a.shape, a.dtype) for a in sources],
        scratch_shapes=[
            pltpu.VMEM((3 * max(len(firsts), 1), channels, plane, width), BF),
            pltpu.SemaphoreType.DMA((3 * max(len(firsts), 1),)),
            pltpu.SemaphoreType.DMA((3,)),
        ],
        name="load",
        compiler_params=PARAMS,
    )(*[in_hbm(a) for a in (*sources, img)])
    scalars = [in_smem(a) for a in (shift_s, frac_s, valid_s)]
    tables = [in_vmem(a) for a in (plane_table, line_table)]

    def send(parts):
        chunks = []
        for d, part in zip(peers, parts, strict=True):
            chunks.append(lax.ppermute(part, "round", [(i, (i + d) % rounds) for i in range(rounds)]))
        return chunks

    def filtered(groups, sums, halo=()):
        ins = [in_vmem(img), *tables, *[in_vmem(a) for a in (*halo, *sums)]]
        return pl.pallas_call(
            functools.partial(filter_kernel, groups, not sums, len(halo)),
            in_specs=[SMEM] * 3 + [VMEM] * len(ins),
            out_specs=[VMEM] * (sum(halves for _, halves in groups) + 1),
            out_shape=[
                out((len(g), channels, plane // halves, width), BF) for g, halves in groups for _ in range(halves)
            ]
            + [sum_shape],
            compiler_params=PARAMS,
        )(*scalars, *ins)

    shifted = send(parts) if early else []
    swaps = pl.pallas_call(
        pack_kernel,
        in_specs=[SMEM, VMEM],
        out_specs=[VMEM] * 2,
        out_shape=[out((plane, width), BF)] * 2,
        name="pack",
        compiler_params=PARAMS,
    )(scalars[2], in_vmem(img))
    halo = []
    for links, swap in zip(swaps_of(count), (swaps[0], swaps[1], swaps[1])):
        halo.append(lax.ppermute(swap, "brick", links))
    sums = []
    if inner:
        *parts, stat = filtered([([pick_for(d, j) for j in inner], 1) for d in peers], sums)
        sums = [stat]
        arrived_inner = send(parts)
    last = quota - 1
    if last:
        own, stat = filtered([([pick_for(0, j) for j in range(last)], 1)], sums)
        sums = [stat]
    groups = [([pick_for(0, last)], 1)] + [([pick_for(d, last)], HALVES) for d in peers]
    own_last, *parts, stat = filtered(groups, sums, halo)
    ins = [*tables, *[in_vmem(a) for a in (stat, *shifted)]]
    *arrived, stat = pl.pallas_call(
        functools.partial(close_kernel, pick_for(0, 0)),
        in_specs=[SMEM] * 3 + [VMEM] * len(ins),
        out_specs=[VMEM] * (len(shifted) + 1),
        out_shape=[out((1, channels, plane, width), BF)] * len(shifted)
        + [jax.ShapeDtypeStruct((rounds * count, 1, width), F32)],
        name="k4",
        compiler_params=PARAMS,
    )(*scalars, *ins)
    stats = lax.all_to_all(stat, ("round", "brick"), split_axis=0, concat_axis=0, tiled=True)

    arrived_last = [send(parts[k::HALVES]) for k in range(HALVES)]

    part = plane // HALVES
    step = plane // CHUNKS

    def task(j, n, keep, arrays):
        if j < last:
            theirs = arrived if j == 0 else arrived_inner
            found = [(own, j, 0)] + [(a, 0 if j == 0 else j - 1, 0) for a in theirs]
        else:
            k = n * step // part
            found = [(own_last, 0, 0)] + [(a, 0, k * part) for a in arrived_last[k]]
        sources = []
        for array, m, base in found:
            if all(array is not a for a in arrays):
                arrays.append(array)
            sources.append(([array is a for a in arrays].index(True), m, base))
        return j, n, sources, keep

    pieces = [(j, n) for j in range(quota) for n in range(CHUNKS)]
    late = pieces[len(pieces) - CHUNKS // HALVES :]
    pieces = pieces[: len(pieces) - len(late)]
    carried = pieces[len(pieces) * 4 // 7 :]
    arrays = []
    tasks = [task(j, n, (j, n) in carried, arrays) for j, n in pieces]
    tile = (rounds, channels, step, width)
    ins = [in_vmem(a) for a in (valid.reshape(1, -1), stats, *arrays)]
    stored = max(len(pieces) - len(carried), 1)
    result, inverse, kept = pl.pallas_call(
        functools.partial(norm1_kernel, rounds, bool(early), tasks),
        in_specs=[VMEM] * len(ins),
        out_specs=[HBM, VMEM, VMEM],
        out_shape=[
            jax.ShapeDtypeStruct((rounds, 1, quota, channels, plane, width), BF),
            out((rounds, channels, 8, width), F32),
            out((len(carried), *tile), BF),
        ],
        scratch_shapes=[pltpu.VMEM((stored, *tile), BF), pltpu.SemaphoreType.DMA((stored, rounds))],
        name="norm1",
        compiler_params=PARAMS,
    )(*ins)
    arrays = []
    tasks = [task(j, n, False, arrays) for j, n in late]
    ins = [in_hbm(result)] + [in_vmem(a) for a in (inverse, kept, *arrays)]
    result = pl.pallas_call(
        functools.partial(norm2_kernel, rounds, tasks, carried),
        in_specs=[HBM] + [VMEM] * (len(ins) - 1),
        out_specs=HBM,
        out_shape=jax.ShapeDtypeStruct(result.shape, BF),
        scratch_shapes=[
            pltpu.VMEM((len(late), *tile), BF),
            pltpu.SemaphoreType.DMA((len(late), rounds)),
            pltpu.SemaphoreType.DMA((len(carried), rounds)),
        ],
        input_output_aliases={0: 0},
        name="norm2",
        compiler_params=PARAMS,
    )(*ins)
    return result.reshape(rounds, 1, quota, channels, depth, height, width)


def solution(mesh):
    in_specs = (
        P("round", "brick", None, None, None, None),
        P("round", "brick"),
        P("round", "brick"),
        P(),
    )
    out_specs = P(None, "round", "brick", None, None, None, None)
    return jax.shard_map(body, mesh=mesh, in_specs=in_specs, out_specs=out_specs, check_vma=False)
```

profile of v0, /device:TPU:0, one launch (start us, length us, event | category | flops | bytes accessed | tf_op | source)
XLA Modules:
  0.0 44.0 jit_solution(6211498207242071488)
XLA Ops:
  0.0 0.0 copy-start
  0.0 1.7 %load.1 = (bf16[1,4,256,128]{3,2,1,0:T(8,128)(2,1)S(1)}, s32[1,8]{1,0:T(1,128)S(4)}, f32[1,8]{1,0:T(1,128)S(4)}, s32[128]{0:T(128)S(4)}) custom-call(s32[1,8]{1,0:T(1,128)} %shift_hbm.1, f32[1,8]{1,0:T(1,128)} %frac_hbm.1, s32[128]{0:T(128)} %valid_hbm.1, bf16[8,4,256,128]{3,2,1,0:T(8,128)(2,1)} %bitcast.5), custom_call_target="tpu_custom_call" | custom-call | tf_op jit(solution)/shard_map/load/pallas_call | solution.py:357
  1.7 0.1 copy-done
  1.8 0.0 copy-start.1
  1.8 1.0 %copy-done.1 = bf16[1024,256]{1,0:T(8,128)(2,1)S(1)} copy-done((bf16[1024,256]{1,0:T(8,128)(2,1)S(1)}, bf16[1024,256]{1,0:T(8,128)(2,1)}, u32[]{:S(2)}) %copy-start.1) | copy-done | bytes 524312
  2.9 0.0 copy-start.2
  2.9 0.9 %copy-done.2 = f32[2,256,128]{2,1,0:T(8,128)S(1)} copy-done((f32[2,256,128]{2,1,0:T(8,128)S(1)}, f32[2,256,128]{2,1,0:T(8,128)}, u32[]{:S(2)}) %copy-start.2) | copy-done | bytes 262168
  3.8 0.0 copy-start.3
  3.8 1.2 %shard_map.64 = (bf16[2,4,256,128]{3,2,1,0:T(8,128)(2,1)S(1)}, f32[4,8,128]{2,1,0:T(8,128)S(1)}) custom-call(s32[1,8]{1,0:T(1,128)S(4)} %get-tuple-element.24.shift_ref, f32[1,8]{1,0:T(1,128)S(4)} %get-tuple-element.25.frac_ref, s32[128]{0:T(128)S(4)} %get-tuple-element.26.valid_ref, bf16[8,4,256,128]{3,2,1,0:T(8,128)(2,1)S(1)} %bitcast.6, ...), custom_call_target="tpu_custom_call" | custom-call | tf_op jit(solution)/shard_map/pallas_call | solution.py:382
  5.1 3.0 %collective-permute-start.4 = (bf16[2,4,256,128]{3,2,1,0:T(8,128)(2,1)S(1)}, bf16[2,4,256,128]{3,2,1,0:T(8,128)(2,1)S(1)}, u32[]{:S(2)}, u32[]{:S(2)}) collective-permute-start(bf16[2,4,256,128]{3,2,1,0:T(8,128)(2,1)S(1)} %get-tuple-element.36), channel_id=1, source_target_pairs={{0,16},{16,0},{1,17},{17,1},{2,18},{18,2},{3,19},{19,3},{4,20},{20... | collective-permute-start | bytes 1572872 | tf_op jit(solution)/shard_map/ppermute | solution.py:377
  8.1 0.1 collective-permute-start.3
  8.2 0.2 pack.1
  8.4 0.1 collective-permute-start
  8.5 0.5 %collective-permute-start.2 = (bf16[256,128]{1,0:T(8,128)(2,1)S(1)}, bf16[256,128]{1,0:T(8,128)(2,1)S(1)}, u32[]{:S(2)}, u32[]{:S(2)}) collective-permute-start(bf16[256,128]{1,0:T(8,128)(2,1)S(1)} %get-tuple-element.28), channel_id=1, source_target_pairs={{3,4},{4,3},{7,8},{8,7},{11,12},{12,11},{5,6},{6,5},{9,10},{10,9},... | collective-permute-start | bytes 196616 | tf_op jit(solution)/shard_map/ppermute | solution.py:404
  9.0 2.8 %collective-permute-start.1 = (bf16[256,128]{1,0:T(8,128)(2,1)S(1)}, bf16[256,128]{1,0:T(8,128)(2,1)S(1)}, u32[]{:S(2)}, u32[]{:S(2)}) collective-permute-start(bf16[256,128]{1,0:T(8,128)(2,1)S(1)} %get-tuple-element.28), channel_id=1, source_target_pairs={{1,2},{2,1},{5,6},{6,5},{9,10},{10,9},{13,14},{14,13},{0,3},{3,0},... | collective-permute-start | bytes 196616 | tf_op jit(solution)/shard_map/ppermute | solution.py:404
  11.8 0.0 copy-done.3
  11.8 1.8 %shard_map.65 = (bf16[3,4,256,128]{3,2,1,0:T(8,128)(2,1)S(1)}, f32[4,8,128]{2,1,0:T(8,128)S(1)}) custom-call(s32[1,8]{1,0:T(1,128)S(4)} %get-tuple-element.24.shift_ref, f32[1,8]{1,0:T(1,128)S(4)} %get-tuple-element.25.frac_ref, s32[128]{0:T(128)S(4)} %get-tuple-element.26.valid_ref, bf16[8,4,256,128]{3,2,1,0:T(8,128)(2,1)S(1)} %bitcast.8, ...), custom_call_target="tpu_custom_call" | custom-call | tf_op jit(solution)/shard_map/pallas_call | solution.py:382
  13.5 0.0 collective-permute-done.refs_0_
  13.5 0.0 collective-permute-done.2.refs_2_
  13.5 0.4 collective-permute-done.1.refs_1_
  13.9 0.0 copy-start.4
  13.9 1.4 %shard_map.66 = (bf16[1,4,256,128]{3,2,1,0:T(8,128)(2,1)S(1)}, bf16[1,4,128,128]{3,2,1,0:T(8,128)(2,1)S(1)}, bf16[1,4,128,128]{3,2,1,0:T(8,128)(2,1)S(1)}, f32[4,8,128]{2,1,0:T(8,128)S(1)}) custom-call(s32[1,8]{1,0:T(1,128)S(4)} %get-tuple-element.24.shift_ref, f32[1,8]{1,0:T(1,128)S(4)} %get-tuple-element.25.frac_ref, s32[128]{0:T(128)S(4)} %get-tuple-element.26.valid_ref, ...), custom_call_target="tpu_custom_call" | custom-call | tf_op jit(solution)/shard_map/pallas_call | solution.py:382
  15.4 1.7 %collective-permute-start.5 = (bf16[1,4,128,128]{3,2,1,0:T(8,128)(2,1)S(1)}, bf16[1,4,128,128]{3,2,1,0:T(8,128)(2,1)S(1)}, u32[]{:S(2)}, u32[]{:S(2)}) collective-permute-start(bf16[1,4,128,128]{3,2,1,0:T(8,128)(2,1)S(1)} %get-tuple-element.38), channel_id=1, source_target_pairs={{0,16},{16,0},{1,17},{17,1},{2,18},{18,2},{3,19},{19,3},{4,20},{20... | collective-permute-start | bytes 393224 | tf_op jit(solution)/shard_map/ppermute | solution.py:377
  17.1 0.4 collective-permute-start.6
  17.5 9.0 %collective-permute-done.3.refs_0_ = bf16[1,4,256,128]{3,2,1,0:T(8,128)(2,1)S(1)} collective-permute-done((bf16[1,4,256,128]{3,2,1,0:T(8,128)(2,1)S(1)}, bf16[1,4,256,128]{3,2,1,0:T(8,128)(2,1)S(1)}, u32[]{:S(2)}, u32[]{:S(2)}) %collective-permute-start.3) | collective-permute-done | bytes 262176 | tf_op jit(solution)/shard_map/ppermute | solution.py:377
  26.5 1.4 %k4.1 = (bf16[1,4,256,128]{3,2,1,0:T(8,128)(2,1)S(1)}, f32[32,1,128]{2,1,0:T(1,128)}) custom-call(s32[1,8]{1,0:T(1,128)S(4)} %get-tuple-element.24.shift_ref, f32[1,8]{1,0:T(1,128)S(4)} %get-tuple-element.25.frac_ref, s32[128]{0:T(128)S(4)} %get-tuple-element.26.valid_ref, bf16[1024,256]{1,0:T(8,128)(2,1)S(1)} %copy-done.1, f32[2,256,128]{2,1,0:T(8,128)S(1)} %copy-done.3, ...), custom_call_target="tpu_custom_call" | custom-call | tf_op jit(solution)/shard_map/k4/pallas_call | solution.py:417
  27.9 6.4 %all-to-all-start = ((f32[32,1,128]{2,1,0:T(1,128)}), f32[32,1,128]{2,1,0:T(1,128)S(1)}, u32[]{:S(2)}, u32[]{:S(2)}) async-start(f32[32,1,128]{2,1,0:T(1,128)} %get-tuple-element.33), calls=%async_computation | async-start | bytes 32768 | tf_op jit(solution)/shard_map/all_to_all | solution.py:426
  34.3 0.0 collective-permute-done.5.refs_4_
  34.3 7.1 %all-to-all-done.stat_ref = f32[32,1,128]{2,1,0:T(1,128)S(1)} async-done(((f32[32,1,128]{2,1,0:T(1,128)}), f32[32,1,128]{2,1,0:T(1,128)S(1)}, u32[]{:S(2)}, u32[]{:S(2)}) %all-to-all-start) | async-done | bytes 16416 | tf_op jit(solution)/shard_map/all_to_all | solution.py:426
  41.4 0.0 collective-permute-done.4.refs_2_
  41.4 0.0 copy-done.4
  41.4 1.5 %norm1.1 = (bf16[2,1,4,4,256,128]{5,4,3,2,1,0:T(8,128)(2,1)}, f32[2,4,8,128]{3,2,1,0:T(8,128)S(1)}, bf16[6,2,4,64,128]{4,3,2,1,0:T(8,128)(2,1)S(1)}) custom-call(s32[1,128]{1,0:T(1,128)S(1)} %bitcast.10, f32[32,1,128]{2,1,0:T(1,128)S(1)} %all-to-all-done.stat_ref, bf16[3,4,256,128]{3,2,1,0:T(8,128)(2,1)S(1)} %get-tuple-element.34.refs_0_, ...), custom_call_target="tpu_custom_call" | custom-call | tf_op jit(solution)/shard_map/norm1/pallas_call | solution.py:456
  42.8 0.0 collective-permute-done.6.refs_1_
  42.9 1.1 %norm2.1 = bf16[2,1,4,4,256,128]{5,4,3,2,1,0:T(8,128)(2,1)} custom-call(bf16[2,1,4,4,256,128]{5,4,3,2,1,0:T(8,128)(2,1)} %get-tuple-element.39.result_ref, f32[2,4,8,128]{3,2,1,0:T(8,128)S(1)} %get-tuple-element.40.inverse_ref, bf16[6,2,4,64,128]{4,3,2,1,0:T(8,128)(2,1)S(1)} %get-tuple-element.41.kept_ref, ...), custom_call_target="tpu_custom_call", output_to_operand_aliasing={{}: (0, {})} | custom-call | tf_op jit(solution)/shard_map/norm2/pallas_call | solution.py:472
Async XLA Ops:
  0.0 1.8 %copy-start = (bf16[1,8,4,32,8,128]{5,4,3,2,1,0:T(8,128)(2,1)S(1)}, bf16[1,8,4,32,8,128]{5,4,3,2,1,0:T(8,128)(2,1)}, u32[]{:S(2)}) copy-start(bf16[1,8,4,32,8,128]{5,4,3,2,1,0:T(8,128)(2,1)} %param.6) | copy-start | bytes 6291460
  1.8 1.0 %copy-start.1 = (bf16[1024,256]{1,0:T(8,128)(2,1)S(1)}, bf16[1024,256]{1,0:T(8,128)(2,1)}, u32[]{:S(2)}) copy-start(bf16[1024,256]{1,0:T(8,128)(2,1)} %constant.4.clone.plane_ref) | copy-start | bytes 1572868
  2.9 0.9 %copy-start.2 = (f32[2,256,128]{2,1,0:T(8,128)S(1)}, f32[2,256,128]{2,1,0:T(8,128)}, u32[]{:S(2)}) copy-start(f32[2,256,128]{2,1,0:T(8,128)} %constant.5.clone.line_ref) | copy-start | bytes 786436
  3.8 7.9 %copy-start.3 = (f32[2,256,128]{2,1,0:T(8,128)S(1)}, f32[2,256,128]{2,1,0:T(8,128)}, u32[]{:S(2)}) copy-start(f32[2,256,128]{2,1,0:T(8,128)} %constant.5.clone.line_ref) | copy-start | bytes 786436
  5.1 36.3 %collective-permute-start.4 = (bf16[2,4,256,128]{3,2,1,0:T(8,128)(2,1)S(1)}, bf16[2,4,256,128]{3,2,1,0:T(8,128)(2,1)S(1)}, u32[]{:S(2)}, u32[]{:S(2)}) collective-permute-start(bf16[2,4,256,128]{3,2,1,0:T(8,128)(2,1)S(1)} %get-tuple-element.36), channel_id=1, source_target_pairs={{0,16},{16,0},{1,17},{17,1},{2,18},{18,2},{3,19},{19,3},{4,20},{20... | collective-permute-start | bytes 1572872 | tf_op jit(solution)/shard_map/ppermute | solution.py:377
  8.1 18.4 %collective-permute-start.3 = (bf16[1,4,256,128]{3,2,1,0:T(8,128)(2,1)S(1)}, bf16[1,4,256,128]{3,2,1,0:T(8,128)(2,1)S(1)}, u32[]{:S(2)}, u32[]{:S(2)}) collective-permute-start(bf16[1,4,256,128]{3,2,1,0:T(8,128)(2,1)S(1)} %get-tuple-element.32), channel_id=1, source_target_pairs={{0,16},{16,0},{1,17},{17,1},{2,18},{18,2},{3,19},{19,3},{4,20},{20... | collective-permute-start | bytes 786440 | tf_op jit(solution)/shard_map/ppermute | solution.py:377
  8.4 5.1 %collective-permute-start = (bf16[256,128]{1,0:T(8,128)(2,1)S(1)}, bf16[256,128]{1,0:T(8,128)(2,1)S(1)}, u32[]{:S(2)}, u32[]{:S(2)}) collective-permute-start(bf16[256,128]{1,0:T(8,128)(2,1)S(1)} %get-tuple-element.27), channel_id=1, source_target_pairs={{0,1},{1,0},{2,3},{3,2},{4,5},{5,4},{6,7},{7,6},{8,9},{9,8},{10,11... | collective-permute-start | bytes 196616 | tf_op jit(solution)/shard_map/ppermute | solution.py:404
  8.5 5.1 %collective-permute-start.2 = (bf16[256,128]{1,0:T(8,128)(2,1)S(1)}, bf16[256,128]{1,0:T(8,128)(2,1)S(1)}, u32[]{:S(2)}, u32[]{:S(2)}) collective-permute-start(bf16[256,128]{1,0:T(8,128)(2,1)S(1)} %get-tuple-element.28), channel_id=1, source_target_pairs={{3,4},{4,3},{7,8},{8,7},{11,12},{12,11},{5,6},{6,5},{9,10},{10,9},... | collective-permute-start | bytes 196616 | tf_op jit(solution)/shard_map/ppermute | solution.py:404
  9.0 5.0 %collective-permute-start.1 = (bf16[256,128]{1,0:T(8,128)(2,1)S(1)}, bf16[256,128]{1,0:T(8,128)(2,1)S(1)}, u32[]{:S(2)}, u32[]{:S(2)}) collective-permute-start(bf16[256,128]{1,0:T(8,128)(2,1)S(1)} %get-tuple-element.28), channel_id=1, source_target_pairs={{1,2},{2,1},{5,6},{6,5},{9,10},{10,9},{13,14},{14,13},{0,3},{3,0},... | collective-permute-start | bytes 196616 | tf_op jit(solution)/shard_map/ppermute | solution.py:404
  13.9 27.4 %copy-start.4 = (s32[128]{0:T(128)S(1)}, s32[128]{0:T(128)}, u32[]{:S(2)}) copy-start(s32[128]{0:T(128)} %valid_hbm.1) | copy-start | bytes 1540
  15.4 18.9 %collective-permute-start.5 = (bf16[1,4,128,128]{3,2,1,0:T(8,128)(2,1)S(1)}, bf16[1,4,128,128]{3,2,1,0:T(8,128)(2,1)S(1)}, u32[]{:S(2)}, u32[]{:S(2)}) collective-permute-start(bf16[1,4,128,128]{3,2,1,0:T(8,128)(2,1)S(1)} %get-tuple-element.38), channel_id=1, source_target_pairs={{0,16},{16,0},{1,17},{17,1},{2,18},{18,2},{3,19},{19,3},{4,20},{20... | collective-permute-start | bytes 393224 | tf_op jit(solution)/shard_map/ppermute | solution.py:377
  17.1 25.7 %collective-permute-start.6 = (bf16[1,4,128,128]{3,2,1,0:T(8,128)(2,1)S(1)}, bf16[1,4,128,128]{3,2,1,0:T(8,128)(2,1)S(1)}, u32[]{:S(2)}, u32[]{:S(2)}) collective-permute-start(bf16[1,4,128,128]{3,2,1,0:T(8,128)(2,1)S(1)} %get-tuple-element.42), channel_id=1, source_target_pairs={{0,16},{16,0},{1,17},{17,1},{2,18},{18,2},{3,19},{19,3},{4,20},{20... | collective-permute-start | bytes 393224 | tf_op jit(solution)/shard_map/ppermute | solution.py:377
  27.9 13.5 %all-to-all-start = ((f32[32,1,128]{2,1,0:T(1,128)}), f32[32,1,128]{2,1,0:T(1,128)S(1)}, u32[]{:S(2)}, u32[]{:S(2)}) async-start(f32[32,1,128]{2,1,0:T(1,128)} %get-tuple-element.33), calls=%async_computation | async-start | bytes 32768 | tf_op jit(solution)/shard_map/all_to_all | solution.py:426
where the time goes:
time: 44.2 us; the launch traced here: 44 us
  waiting for transfers between devices  16.5 us (37%)
  starting transfers between devices  14.9 us (34%)
  Pallas kernels  10.3 us (23%)
  local copies, waits for them, and re-layouts  2.08 us (5%)
    ppermute x4, waiting for transfers between devices, send(): lax.ppermute(part, 'round', [(i, (i + d) % rounds) for i in range(rounds)])  9.02 us
    all_to_all x1, waiting for transfers between devices, body(): lax.all_to_all(stat, ('round', 'brick'), split_axis=0, concat_axis=0, til...  7.09 us
    all_to_all x1, starting transfers between devices, body(): lax.all_to_all(stat, ('round', 'brick'), split_axis=0, concat_axis=0, til...  6.38 us
    ppermute x4, starting transfers between devices, send(): lax.ppermute(part, 'round', [(i, (i + d) % rounds) for i in range(rounds)])  5.2 us
    pallas_call x3, Pallas kernels, filtered(): pl.pallas_call(functools.partial(filter_kernel, groups, not sums, len(hal...  4.44 us
    ppermute x3, starting transfers between devices, body(): halo.append(lax.ppermute(swap, 'brick', links))  3.34 us
    unnamed x10, local copies, waits for them, and re-layouts  2.08 us
    pallas_call x1, Pallas kernels, body(): pl.pallas_call(functools.partial(load_kernel, firsts), in_specs=[HBM] * 4...  1.73 us
  transfers between devices with their start and end apart: 8, of which 3 were waited for; matrix products, arithmetic and copies ran while one was open for 0% of the time, Pallas kernels for 14%

commit v1 on v0

--- a/solution.py
+++ b/solution.py
@@ -18,6 +18,7 @@
 HBM = pl.BlockSpec(memory_space=pltpu.HBM)
 CHUNKS = 4
 HALVES = 2
+ROWS = 16
 PARAMS = pltpu.CompilerParams(vmem_limit_bytes=24 * 2**20)
 
 
@@ -119,6 +120,10 @@
         gain0 = (1.0 - f) * jnp.where(own0, own_valid, nb_valid)
         gain1 = f * jnp.where(own1, own_valid, nb_valid)
         own0, own1 = (jnp.broadcast_to(m, tiles) for m in (own0, own1))
+        if turned:
+            row = lax.broadcasted_iota(jnp.int32, (width, width), 0) + self.turn_of(b)
+            row = jnp.where(row >= width, row - width, row)
+            turn = (row == lanes_of((width, width))).astype(F32).astype(BF)
         parts = []
         for c in range(channels):
             own = self.img[at(b), c].astype(F32).reshape(tiles)
@@ -128,10 +133,10 @@
                 other = jnp.where(nb == nb_in, other, moved)
             here = jnp.where(own0, own, other) * gain0
             there = jnp.where(own1, own, other) * gain1
-            value = here + pltpu.roll(there, 1, 2)
+            value = (here + pltpu.roll(there, 1, 2)).reshape(plane, width).astype(BF)
             if turned:
-                value = pltpu.roll(value, self.turn_of(b), 2)
-            parts.append(value.reshape(plane, width).astype(BF))
+                value = jnp.dot(value, turn, preferred_element_type=F32).astype(BF)
+            parts.append(value)
         return parts
 
     def turn_of(self, b):
@@ -204,12 +209,16 @@
     swap1_ref[...] = pack(valid_ref, img_ref, jnp.logical_not(even))
 
 
-def filter_kernel(groups, first, edge, shift_ref, frac_ref, valid_ref, img_ref, plane_ref, line_ref, *refs):
+def filter_kernel(groups, first, edge, ahead, behind, shift_ref, frac_ref, valid_ref, img_ref, plane_ref, line_ref, *refs):
     sums_ref = None
     halo, refs = refs[:edge], refs[edge:]
     if not first:
         sums_ref, refs = refs[0], refs[1:]
+    if behind:
+        field_ref, refs = refs[0], refs[1:]
     *out_refs, stat_ref = refs
+    if ahead:
+        *out_refs, next_ref = out_refs
     _, channels, _, width = img_ref.shape
     rank = lax.axis_index("round")
     one = Filter(shift_ref, frac_ref, valid_ref, img_ref, plane_ref, line_ref, halo)
@@ -217,7 +226,16 @@
     for picks, halves in groups:
         refs, out_refs = out_refs[:halves], out_refs[halves:]
         for n, pick in enumerate(picks):
-            totals = one(pick(rank), put_in(refs, n), totals)
+            b = pick(rank)
+            if behind:
+                parts = [field_ref[c] for c in range(channels)]
+                totals = one.apply(parts, one.turn_of(b), put_in(refs, n), totals, one.valid_of(b))
+            else:
+                totals = one(b, put_in(refs, n), totals)
+            behind = False
+    if ahead:
+        for c, part in enumerate(one.field(ahead(rank), lambda n: n, False)):
+            next_ref[c] = part
     for c in range(channels):
         stat_ref[c] = totals[c]
 
@@ -243,26 +261,27 @@
 def norm_kernel(rounds, tasks, out_ref, inverse_ref, data_refs, buf_refs, kept_ref, sem):
     _, channels, plane, width = out_ref.shape[2:]
     step = plane // CHUNKS
-    tiles = (step // 8, 8, width)
+    tiles = (ROWS // 8, 8, width)
     copies = []
     stored, kept = 0, 0
     for j, n, sources, keep in tasks:
-
-        def ratio(d, c):
-            g, m, base = sources[d]
-            data = data_refs[g][m, c, n * step - base : (n + 1) * step - base]
-            return data.astype(F32).reshape(tiles) * inverse_ref[d, c]
-
-        energy = jnp.zeros(tiles, F32)
-        for d in range(rounds):
-            for c in range(channels):
-                part = ratio(d, c)
-                energy = energy + part * part
-        factor = lax.rsqrt(energy * (1.0 / (rounds * channels)) + 1.0)
         to_ref, m = (kept_ref, kept) if keep else (buf_refs, stored)
-        for d in range(rounds):
-            for c in range(channels):
-                to_ref[m, d, c] = (ratio(d, c) * factor).reshape(step, width).astype(BF)
+        for first in range(0, step, ROWS):
+            ratios = []
+            energy = jnp.zeros(tiles, F32)
+            for d in range(rounds):
+                g, k, base = sources[d]
+                begin = n * step - base + first
+                for c in range(channels):
+                    data = data_refs[g][k, c, begin : begin + ROWS]
+                    ratio = data.astype(F32).reshape(tiles) * inverse_ref[d, c]
+                    energy = energy + ratio * ratio
+                    ratios.append(ratio)
+            factor = lax.rsqrt(energy * (1.0 / (rounds * channels)) + 1.0)
+            for d in range(rounds):
+                for c in range(channels):
+                    value = (ratios[d * channels + c] * factor).reshape(ROWS, width).astype(BF)
+                    to_ref[m, d, c, first : first + ROWS] = value
         if keep:
             kept += 1
         else:
@@ -377,15 +396,16 @@
             chunks.append(lax.ppermute(part, "round", [(i, (i + d) % rounds) for i in range(rounds)]))
         return chunks
 
-    def filtered(groups, sums, halo=()):
-        ins = [in_vmem(img), *tables, *[in_vmem(a) for a in (*halo, *sums)]]
+    def filtered(groups, sums, halo=(), ahead=None, field=()):
+        ins = [in_vmem(img), *tables, *[in_vmem(a) for a in (*halo, *sums, *field)]]
         return pl.pallas_call(
-            functools.partial(filter_kernel, groups, not sums, len(halo)),
+            functools.partial(filter_kernel, groups, not sums, len(halo), ahead, bool(field)),
             in_specs=[SMEM] * 3 + [VMEM] * len(ins),
-            out_specs=[VMEM] * (sum(halves for _, halves in groups) + 1),
+            out_specs=[VMEM] * (sum(halves for _, halves in groups) + bool(ahead) + 1),
             out_shape=[
                 out((len(g), channels, plane // halves, width), BF) for g, halves in groups for _ in range(halves)
             ]
+            + [out(img.shape[1:], BF)] * bool(ahead)
             + [sum_shape],
             compiler_params=PARAMS,
         )(*scalars, *ins)
@@ -402,14 +422,16 @@
     halo = []
     for links, swap in zip(swaps_of(count), (swaps[0], swaps[1], swaps[1])):
         halo.append(lax.ppermute(swap, "brick", links))
-    sums = []
+    sums, fields = [], []
     if inner:
-        *parts, stat = filtered([([pick_for(d, j) for j in inner], 1) for d in peers], sums)
+        groups = [([pick_for(d, j) for j in inner], 1) for d in peers]
+        *parts, field, stat = filtered(groups, sums, ahead=pick_for(0, 0))
+        fields = [field]
         sums = [stat]
         arrived_inner = send(parts)
     last = quota - 1
     if last:
-        own, stat = filtered([([pick_for(0, j) for j in range(last)], 1)], sums)
+        own, stat = filtered([([pick_for(0, j) for j in range(last)], 1)], sums, field=fields)
         sums = [stat]
     groups = [([pick_for(0, last)], 1)] + [([pick_for(d, last)], HALVES) for d in peers]
     own_last, *parts, stat = filtered(groups, sums, halo)
@@ -447,7 +469,7 @@
     pieces = [(j, n) for j in range(quota) for n in range(CHUNKS)]
     late = pieces[len(pieces) - CHUNKS // HALVES :]
     pieces = pieces[: len(pieces) - len(late)]
-    carried = pieces[len(pieces) * 4 // 7 :]
+    carried = pieces[len(pieces) * 6 // 7 :]
     arrays = []
     tasks = [task(j, n, (j, n) in carried, arrays) for j, n in pieces]
     tile = (rounds, channels, step, width)

time: 44.2 us -> 44.3 us (level)
  transfers between devices with their start and end apart: 8 -> 8, of which waited for: 3 -> 3; matrix products, arithmetic and copies ran while one was open for 0% -> 0% of each run, Pallas kernels for 14% -> 15%
where the time goes in v1:
time: 44.3 us; the launch traced here: 44 us
  waiting for transfers between devices  16.6 us (37%)
  starting transfers between devices  14.9 us (34%)
  Pallas kernels  10.2 us (23%)
  local copies, waits for them, and re-layouts  2.17 us (5%)
    ppermute x4, waiting for transfers between devices, send(): lax.ppermute(part, 'round', [(i, (i + d) % rounds) for i in range(rounds)])  9.02 us
    all_to_all x1, waiting for transfers between devices, body(): lax.all_to_all(stat, ('round', 'brick'), split_axis=0, concat_axis=0, til...  7.09 us
    all_to_all x1, starting transfers between devices, body(): lax.all_to_all(stat, ('round', 'brick'), split_axis=0, concat_axis=0, til...  6.39 us
    ppermute x4, starting transfers between devices, send(): lax.ppermute(part, 'round', [(i, (i + d) % rounds) for i in range(rounds)])  5.2 us
    pallas_call x3, Pallas kernels, filtered(): pl.pallas_call(functools.partial(filter_kernel, groups, not sums, len(hal...  4.4 us
    ppermute x3, starting transfers between devices, body(): halo.append(lax.ppermute(swap, 'brick', links))  3.34 us
    unnamed x10, local copies, waits for them, and re-layouts  2.17 us
    pallas_call x1, Pallas kernels, body(): pl.pallas_call(functools.partial(norm1_kernel, rounds, bool(early), tasks...  1.7 us
  transfers between devices with their start and end apart: 8, of which 3 were waited for; matrix products, arithmetic and copies ran while one was open for 0% of the time, Pallas kernels for 15%

profile of v1, /device:TPU:0, one launch (start us, length us, event | category | flops | bytes accessed | tf_op | source)
XLA Modules:
  0.0 44.0 jit_solution(17747948057696603549)
XLA Ops:
  0.0 0.0 copy-start
  0.0 1.6 %load.1 = (bf16[1,4,256,128]{3,2,1,0:T(8,128)(2,1)S(1)}, s32[1,8]{1,0:T(1,128)S(4)}, f32[1,8]{1,0:T(1,128)S(4)}, s32[128]{0:T(128)S(4)}) custom-call(s32[1,8]{1,0:T(1,128)} %shift_hbm.1, f32[1,8]{1,0:T(1,128)} %frac_hbm.1, s32[128]{0:T(128)} %valid_hbm.1, bf16[8,4,256,128]{3,2,1,0:T(8,128)(2,1)} %bitcast.5), custom_call_target="tpu_custom_call" | custom-call | tf_op jit(solution)/shard_map/load/pallas_call | solution.py:376
  1.7 0.2 copy-done
  1.8 0.0 copy-start.1
  1.8 1.0 %copy-done.1 = bf16[1024,256]{1,0:T(8,128)(2,1)S(1)} copy-done((bf16[1024,256]{1,0:T(8,128)(2,1)S(1)}, bf16[1024,256]{1,0:T(8,128)(2,1)}, u32[]{:S(2)}) %copy-start.1) | copy-done | bytes 524312
  2.9 0.0 copy-start.2
  2.9 0.9 %copy-done.2 = f32[2,256,128]{2,1,0:T(8,128)S(1)} copy-done((f32[2,256,128]{2,1,0:T(8,128)S(1)}, f32[2,256,128]{2,1,0:T(8,128)}, u32[]{:S(2)}) %copy-start.2) | copy-done | bytes 262168
  3.8 0.0 copy-start.3
  3.8 1.3 %shard_map.64 = (bf16[2,4,256,128]{3,2,1,0:T(8,128)(2,1)S(1)}, bf16[4,256,128]{2,1,0:T(8,128)(2,1)S(1)}, f32[4,8,128]{2,1,0:T(8,128)S(1)}) custom-call(s32[1,8]{1,0:T(1,128)S(4)} %get-tuple-element.25.shift_ref, f32[1,8]{1,0:T(1,128)S(4)} %get-tuple-element.26.frac_ref, s32[128]{0:T(128)S(4)} %get-tuple-element.27.valid_ref, ...), custom_call_target="tpu_custom_call" | custom-call | tf_op jit(solution)/shard_map/pallas_call | solution.py:401
  5.1 3.0 %collective-permute-start.4 = (bf16[2,4,256,128]{3,2,1,0:T(8,128)(2,1)S(1)}, bf16[2,4,256,128]{3,2,1,0:T(8,128)(2,1)S(1)}, u32[]{:S(2)}, u32[]{:S(2)}) collective-permute-start(bf16[2,4,256,128]{3,2,1,0:T(8,128)(2,1)S(1)} %get-tuple-element.38), channel_id=1, source_target_pairs={{0,16},{16,0},{1,17},{17,1},{2,18},{18,2},{3,19},{19,3},{4,20},{20... | collective-permute-start | bytes 1572872 | tf_op jit(solution)/shard_map/ppermute | solution.py:396
  8.2 0.1 collective-permute-start.3
  8.2 0.2 pack.1
  8.4 0.1 collective-permute-start
  8.5 0.5 %collective-permute-start.2 = (bf16[256,128]{1,0:T(8,128)(2,1)S(1)}, bf16[256,128]{1,0:T(8,128)(2,1)S(1)}, u32[]{:S(2)}, u32[]{:S(2)}) collective-permute-start(bf16[256,128]{1,0:T(8,128)(2,1)S(1)} %get-tuple-element.29), channel_id=1, source_target_pairs={{3,4},{4,3},{7,8},{8,7},{11,12},{12,11},{5,6},{6,5},{9,10},{10,9},... | collective-permute-start | bytes 196616 | tf_op jit(solution)/shard_map/ppermute | solution.py:424
  9.0 2.8 %collective-permute-start.1 = (bf16[256,128]{1,0:T(8,128)(2,1)S(1)}, bf16[256,128]{1,0:T(8,128)(2,1)S(1)}, u32[]{:S(2)}, u32[]{:S(2)}) collective-permute-start(bf16[256,128]{1,0:T(8,128)(2,1)S(1)} %get-tuple-element.29), channel_id=1, source_target_pairs={{1,2},{2,1},{5,6},{6,5},{9,10},{10,9},{13,14},{14,13},{0,3},{3,0},... | collective-permute-start | bytes 196616 | tf_op jit(solution)/shard_map/ppermute | solution.py:424
  11.8 0.0 copy-done.3
  11.8 1.7 %shard_map.65 = (bf16[3,4,256,128]{3,2,1,0:T(8,128)(2,1)S(1)}, f32[4,8,128]{2,1,0:T(8,128)S(1)}) custom-call(s32[1,8]{1,0:T(1,128)S(4)} %get-tuple-element.25.shift_ref, f32[1,8]{1,0:T(1,128)S(4)} %get-tuple-element.26.frac_ref, s32[128]{0:T(128)S(4)} %get-tuple-element.27.valid_ref, bf16[8,4,256,128]{3,2,1,0:T(8,128)(2,1)S(1)} %bitcast.8, ...), custom_call_target="tpu_custom_call" | custom-call | tf_op jit(solution)/shard_map/pallas_call | solution.py:401
  13.5 0.0 collective-permute-done.refs_0_
  13.5 0.0 collective-permute-done.2.refs_2_
  13.5 0.5 %collective-permute-done.1.refs_1_ = bf16[256,128]{1,0:T(8,128)(2,1)S(1)} collective-permute-done((bf16[256,128]{1,0:T(8,128)(2,1)S(1)}, bf16[256,128]{1,0:T(8,128)(2,1)S(1)}, u32[]{:S(2)}, u32[]{:S(2)}) %collective-permute-start.1) | collective-permute-done | bytes 65568 | tf_op jit(solution)/shard_map/ppermute | solution.py:424
  14.0 0.0 copy-start.4
  14.0 1.4 %shard_map.66 = (bf16[1,4,256,128]{3,2,1,0:T(8,128)(2,1)S(1)}, bf16[1,4,128,128]{3,2,1,0:T(8,128)(2,1)S(1)}, bf16[1,4,128,128]{3,2,1,0:T(8,128)(2,1)S(1)}, f32[4,8,128]{2,1,0:T(8,128)S(1)}) custom-call(s32[1,8]{1,0:T(1,128)S(4)} %get-tuple-element.25.shift_ref, f32[1,8]{1,0:T(1,128)S(4)} %get-tuple-element.26.frac_ref, s32[128]{0:T(128)S(4)} %get-tuple-element.27.valid_ref, ...), custom_call_target="tpu_custom_call" | custom-call | tf_op jit(solution)/shard_map/pallas_call | solution.py:401
  15.4 1.7 %collective-permute-start.5 = (bf16[1,4,128,128]{3,2,1,0:T(8,128)(2,1)S(1)}, bf16[1,4,128,128]{3,2,1,0:T(8,128)(2,1)S(1)}, u32[]{:S(2)}, u32[]{:S(2)}) collective-permute-start(bf16[1,4,128,128]{3,2,1,0:T(8,128)(2,1)S(1)} %get-tuple-element.40), channel_id=1, source_target_pairs={{0,16},{16,0},{1,17},{17,1},{2,18},{18,2},{3,19},{19,3},{4,20},{20... | collective-permute-start | bytes 393224 | tf_op jit(solution)/shard_map/ppermute | solution.py:396
  17.2 0.4 collective-permute-start.6
  17.5 9.0 %collective-permute-done.3.refs_0_ = bf16[1,4,256,128]{3,2,1,0:T(8,128)(2,1)S(1)} collective-permute-done((bf16[1,4,256,128]{3,2,1,0:T(8,128)(2,1)S(1)}, bf16[1,4,256,128]{3,2,1,0:T(8,128)(2,1)S(1)}, u32[]{:S(2)}, u32[]{:S(2)}) %collective-permute-start.3) | collective-permute-done | bytes 262176 | tf_op jit(solution)/shard_map/ppermute | solution.py:396
  26.5 1.4 %k4.1 = (bf16[1,4,256,128]{3,2,1,0:T(8,128)(2,1)S(1)}, f32[32,1,128]{2,1,0:T(1,128)}) custom-call(s32[1,8]{1,0:T(1,128)S(4)} %get-tuple-element.25.shift_ref, f32[1,8]{1,0:T(1,128)S(4)} %get-tuple-element.26.frac_ref, s32[128]{0:T(128)S(4)} %get-tuple-element.27.valid_ref, bf16[1024,256]{1,0:T(8,128)(2,1)S(1)} %copy-done.1, f32[2,256,128]{2,1,0:T(8,128)S(1)} %copy-done.3, ...), custom_call_target="tpu_custom_call" | custom-call | tf_op jit(solution)/shard_map/k4/pallas_call | solution.py:439
  27.9 6.4 %all-to-all-start = ((f32[32,1,128]{2,1,0:T(1,128)}), f32[32,1,128]{2,1,0:T(1,128)S(1)}, u32[]{:S(2)}, u32[]{:S(2)}) async-start(f32[32,1,128]{2,1,0:T(1,128)} %get-tuple-element.35), calls=%async_computation | async-start | bytes 32768 | tf_op jit(solution)/shard_map/all_to_all | solution.py:448
  34.3 0.0 collective-permute-done.5.refs_4_
  34.3 7.1 %all-to-all-done.stat_ref = f32[32,1,128]{2,1,0:T(1,128)S(1)} async-done(((f32[32,1,128]{2,1,0:T(1,128)}), f32[32,1,128]{2,1,0:T(1,128)S(1)}, u32[]{:S(2)}, u32[]{:S(2)}) %all-to-all-start) | async-done | bytes 16416 | tf_op jit(solution)/shard_map/all_to_all | solution.py:448
  41.4 0.0 collective-permute-done.4.refs_2_
  41.4 0.0 copy-done.4
  41.4 1.7 %norm1.1 = (bf16[2,1,4,4,256,128]{5,4,3,2,1,0:T(8,128)(2,1)}, f32[2,4,8,128]{3,2,1,0:T(8,128)S(1)}, bf16[2,2,4,64,128]{4,3,2,1,0:T(8,128)(2,1)S(1)}) custom-call(s32[1,128]{1,0:T(1,128)S(1)} %bitcast.10, f32[32,1,128]{2,1,0:T(1,128)S(1)} %all-to-all-done.stat_ref, bf16[3,4,256,128]{3,2,1,0:T(8,128)(2,1)S(1)} %get-tuple-element.36.refs_0_, ...), custom_call_target="tpu_custom_call" | custom-call | tf_op jit(solution)/shard_map/norm1/pallas_call | solution.py:478
  43.1 0.0 collective-permute-done.6.refs_1_
  43.1 0.9 %norm2.1 = bf16[2,1,4,4,256,128]{5,4,3,2,1,0:T(8,128)(2,1)} custom-call(bf16[2,1,4,4,256,128]{5,4,3,2,1,0:T(8,128)(2,1)} %get-tuple-element.41.result_ref, f32[2,4,8,128]{3,2,1,0:T(8,128)S(1)} %get-tuple-element.42.inverse_ref, bf16[2,2,4,64,128]{4,3,2,1,0:T(8,128)(2,1)S(1)} %get-tuple-element.43.kept_ref, ...), custom_call_target="tpu_custom_call", output_to_operand_aliasing={{}: (0, {})} | custom-call | tf_op jit(solution)/shard_map/norm2/pallas_call | solution.py:494
Async XLA Ops:
  0.0 1.8 %copy-start = (bf16[1,8,4,32,8,128]{5,4,3,2,1,0:T(8,128)(2,1)S(1)}, bf16[1,8,4,32,8,128]{5,4,3,2,1,0:T(8,128)(2,1)}, u32[]{:S(2)}) copy-start(bf16[1,8,4,32,8,128]{5,4,3,2,1,0:T(8,128)(2,1)} %param.6) | copy-start | bytes 6291460
  1.8 1.0 %copy-start.1 = (bf16[1024,256]{1,0:T(8,128)(2,1)S(1)}, bf16[1024,256]{1,0:T(8,128)(2,1)}, u32[]{:S(2)}) copy-start(bf16[1024,256]{1,0:T(8,128)(2,1)} %constant.4.clone.plane_ref) | copy-start | bytes 1572868
  2.9 0.9 %copy-start.2 = (f32[2,256,128]{2,1,0:T(8,128)S(1)}, f32[2,256,128]{2,1,0:T(8,128)}, u32[]{:S(2)}) copy-start(f32[2,256,128]{2,1,0:T(8,128)} %constant.5.clone.line_ref) | copy-start | bytes 786436
  3.8 8.0 %copy-start.3 = (f32[2,256,128]{2,1,0:T(8,128)S(1)}, f32[2,256,128]{2,1,0:T(8,128)}, u32[]{:S(2)}) copy-start(f32[2,256,128]{2,1,0:T(8,128)} %constant.5.clone.line_ref) | copy-start | bytes 786436
  5.1 36.3 %collective-permute-start.4 = (bf16[2,4,256,128]{3,2,1,0:T(8,128)(2,1)S(1)}, bf16[2,4,256,128]{3,2,1,0:T(8,128)(2,1)S(1)}, u32[]{:S(2)}, u32[]{:S(2)}) collective-permute-start(bf16[2,4,256,128]{3,2,1,0:T(8,128)(2,1)S(1)} %get-tuple-element.38), channel_id=1, source_target_pairs={{0,16},{16,0},{1,17},{17,1},{2,18},{18,2},{3,19},{19,3},{4,20},{20... | collective-permute-start | bytes 1572872 | tf_op jit(solution)/shard_map/ppermute | solution.py:396
  8.2 18.4 %collective-permute-start.3 = (bf16[1,4,256,128]{3,2,1,0:T(8,128)(2,1)S(1)}, bf16[1,4,256,128]{3,2,1,0:T(8,128)(2,1)S(1)}, u32[]{:S(2)}, u32[]{:S(2)}) collective-permute-start(bf16[1,4,256,128]{3,2,1,0:T(8,128)(2,1)S(1)} %get-tuple-element.34), channel_id=1, source_target_pairs={{0,16},{16,0},{1,17},{17,1},{2,18},{18,2},{3,19},{19,3},{4,20},{20... | collective-permute-start | bytes 786440 | tf_op jit(solution)/shard_map/ppermute | solution.py:396
  8.4 5.0 %collective-permute-start = (bf16[256,128]{1,0:T(8,128)(2,1)S(1)}, bf16[256,128]{1,0:T(8,128)(2,1)S(1)}, u32[]{:S(2)}, u32[]{:S(2)}) collective-permute-start(bf16[256,128]{1,0:T(8,128)(2,1)S(1)} %get-tuple-element.28), channel_id=1, source_target_pairs={{0,1},{1,0},{2,3},{3,2},{4,5},{5,4},{6,7},{7,6},{8,9},{9,8},{10,11... | collective-permute-start | bytes 196616 | tf_op jit(solution)/shard_map/ppermute | solution.py:424
  8.5 5.0 %collective-permute-start.2 = (bf16[256,128]{1,0:T(8,128)(2,1)S(1)}, bf16[256,128]{1,0:T(8,128)(2,1)S(1)}, u32[]{:S(2)}, u32[]{:S(2)}) collective-permute-start(bf16[256,128]{1,0:T(8,128)(2,1)S(1)} %get-tuple-element.29), channel_id=1, source_target_pairs={{3,4},{4,3},{7,8},{8,7},{11,12},{12,11},{5,6},{6,5},{9,10},{10,9},... | collective-permute-start | bytes 196616 | tf_op jit(solution)/shard_map/ppermute | solution.py:424
  9.0 5.0 %collective-permute-start.1 = (bf16[256,128]{1,0:T(8,128)(2,1)S(1)}, bf16[256,128]{1,0:T(8,128)(2,1)S(1)}, u32[]{:S(2)}, u32[]{:S(2)}) collective-permute-start(bf16[256,128]{1,0:T(8,128)(2,1)S(1)} %get-tuple-element.29), channel_id=1, source_target_pairs={{1,2},{2,1},{5,6},{6,5},{9,10},{10,9},{13,14},{14,13},{0,3},{3,0},... | collective-permute-start | bytes 196616 | tf_op jit(solution)/shard_map/ppermute | solution.py:424
  14.0 27.4 %copy-start.4 = (s32[128]{0:T(128)S(1)}, s32[128]{0:T(128)}, u32[]{:S(2)}) copy-start(s32[128]{0:T(128)} %valid_hbm.1) | copy-start | bytes 1540
  15.4 18.9 %collective-permute-start.5 = (bf16[1,4,128,128]{3,2,1,0:T(8,128)(2,1)S(1)}, bf16[1,4,128,128]{3,2,1,0:T(8,128)(2,1)S(1)}, u32[]{:S(2)}, u32[]{:S(2)}) collective-permute-start(bf16[1,4,128,128]{3,2,1,0:T(8,128)(2,1)S(1)} %get-tuple-element.40), channel_id=1, source_target_pairs={{0,16},{16,0},{1,17},{17,1},{2,18},{18,2},{3,19},{19,3},{4,20},{20... | collective-permute-start | bytes 393224 | tf_op jit(solution)/shard_map/ppermute | solution.py:396
  17.2 26.0 %collective-permute-start.6 = (bf16[1,4,128,128]{3,2,1,0:T(8,128)(2,1)S(1)}, bf16[1,4,128,128]{3,2,1,0:T(8,128)(2,1)S(1)}, u32[]{:S(2)}, u32[]{:S(2)}) collective-permute-start(bf16[1,4,128,128]{3,2,1,0:T(8,128)(2,1)S(1)} %get-tuple-element.44), channel_id=1, source_target_pairs={{0,16},{16,0},{1,17},{17,1},{2,18},{18,2},{3,19},{19,3},{4,20},{20... | collective-permute-start | bytes 393224 | tf_op jit(solution)/shard_map/ppermute | solution.py:396
  27.9 13.5 %all-to-all-start = ((f32[32,1,128]{2,1,0:T(1,128)}), f32[32,1,128]{2,1,0:T(1,128)S(1)}, u32[]{:S(2)}, u32[]{:S(2)}) async-start(f32[32,1,128]{2,1,0:T(1,128)} %get-tuple-element.35), calls=%async_computation | async-start | bytes 32768 | tf_op jit(solution)/shard_map/all_to_all | solution.py:448

commit v2 on v1

--- a/solution.py
+++ b/solution.py
@@ -89,7 +89,7 @@
     def valid_of(self, b):
         return self.valid[lax.axis_index("brick") * self.shift.shape[1] + b].astype(F32)
 
-    def field(self, b, at, turned):
+    def field(self, b):
         bricks = self.shift.shape[1]
         _, channels, plane, width = self.img.shape
         slot = width // channels
@@ -120,24 +120,40 @@
         gain0 = (1.0 - f) * jnp.where(own0, own_valid, nb_valid)
         gain1 = f * jnp.where(own1, own_valid, nb_valid)
         own0, own1 = (jnp.broadcast_to(m, tiles) for m in (own0, own1))
-        if turned:
-            row = lax.broadcasted_iota(jnp.int32, (width, width), 0) + self.turn_of(b)
-            row = jnp.where(row >= width, row - width, row)
-            turn = (row == lanes_of((width, width))).astype(F32).astype(BF)
         parts = []
         for c in range(channels):
-            own = self.img[at(b), c].astype(F32).reshape(tiles)
-            other = self.img[at(nb_in), c].astype(F32).reshape(tiles)
+            own = self.img[b, c].astype(F32).reshape(tiles)
+            other = self.img[nb_in, c].astype(F32).reshape(tiles)
             if self.halo:
                 moved = pltpu.roll(halo, lax.rem(start + (width - c * slot), width), 2)
                 other = jnp.where(nb == nb_in, other, moved)
             here = jnp.where(own0, own, other) * gain0
             there = jnp.where(own1, own, other) * gain1
             value = (here + pltpu.roll(there, 1, 2)).reshape(plane, width).astype(BF)
-            if turned:
-                value = jnp.dot(value, turn, preferred_element_type=F32).astype(BF)
             parts.append(value)
         return parts
+
+    def weights(self, b):
+        width = self.img.shape[-1]
+        s = self.shift[0, b]
+        f = self.frac[0, b]
+        right = s >= 0
+        own_valid = self.valid_of(b)
+        nb_valid = self.valid_of(jnp.where(right, b - 1, b + 1))
+        row = lax.broadcasted_iota(jnp.int32, (width, width), 0)
+        lane = lanes_of((width, width))
+        mine, theirs = jnp.zeros((width, width), F32), jnp.zeros((width, width), F32)
+        for step, gain in ((s, 1.0 - f), (s + 1, f)):
+            low, high = jnp.where(right, 0, -step), jnp.where(right, width - step, width)
+            inside = (row >= low) & (row < high)
+            to = row + step
+            to = jnp.where(to < 0, to + width, jnp.where(to >= width, to - width, to))
+            mine = mine + jnp.where(inside & (to == lane), gain * own_valid, 0.0)
+            theirs = theirs + jnp.where(jnp.logical_not(inside) & (to == lane), gain * nb_valid, 0.0)
+        table = jnp.concatenate([mine, theirs], axis=0)
+        high = table.astype(BF)
+        low = (table - high.astype(F32)).astype(BF)
+        return jnp.concatenate([high, low], axis=1)
 
     def turn_of(self, b):
         s = self.shift[0, b]
@@ -167,7 +183,7 @@
         return added
 
     def __call__(self, b, put, totals):
-        parts = self.field(b, lambda n: n, False)
+        parts = self.field(b)
         return self.apply(parts, self.turn_of(b), put, totals, self.valid_of(b))
 
 
@@ -194,13 +210,19 @@
             copies.append(pltpu.make_async_copy(img_ref.at[b], near_ref.at[3 * k + n], near_sem.at[3 * k + n]))
     for copy in copies:
         copy.start()
-    for copy in copies:
+    for copy in copies[:3]:
         copy.wait()
     one = Filter(shift_ref, frac_ref, valid_ref, near_ref)
+    weights = [one.weights(base + 1) for base in bases]
+    for copy in copies[3:]:
+        copy.wait()
     for k, (base, part_ref) in enumerate(zip(bases, part_refs, strict=True)):
-        parts = one.field(base + 1, lambda n, k=k, base=base: n - base + 3 * k, True)
-        for c, part in enumerate(parts):
-            part_ref[0, c] = part
+        side = jnp.where(shift_ref[0, base + 1] >= 0, 0, 2)
+        for c in range(img_ref.shape[1]):
+            both = jnp.concatenate([near_ref[3 * k + 1, c], near_ref[3 * k + side, c]], axis=1)
+            terms = jnp.dot(both, weights[k], preferred_element_type=F32)
+            width = terms.shape[1] // 2
+            part_ref[0, c] = (terms[:, :width] + terms[:, width:]).astype(BF)
 
 
 def pack_kernel(valid_ref, img_ref, swap0_ref, swap1_ref):
@@ -234,7 +256,7 @@
                 totals = one(b, put_in(refs, n), totals)
             behind = False
     if ahead:
-        for c, part in enumerate(one.field(ahead(rank), lambda n: n, False)):
+        for c, part in enumerate(one.field(ahead(rank))):
             next_ref[c] = part
     for c in range(channels):
         stat_ref[c] = totals[c]
@@ -311,15 +333,23 @@
     rank = lax.axis_index("round")
     count = jnp.maximum(jnp.sum(valid_ref[...]).astype(F32), 1.0)
     each = stat_ref.shape[0] // rounds
+    sums = [jnp.sum(stat_ref[q * each : (q + 1) * each], axis=0) for q in range(rounds)]
+    wide = {
+        (q, e, c): jnp.broadcast_to(sums[q][:, e * channels + c : e * channels + c + 1], (8, width))
+        for q in range(rounds)
+        for e in range(rounds if shared else 1)
+        for c in range(channels)
+    }
     for d in range(rounds):
         slot = lax.rem(rank + rounds - d, rounds)
-        total = jnp.zeros(stat_ref.shape[1:], F32)
-        for e in range(rounds if shared else 1):
-            part = jnp.sum(stat_ref[pl.ds(lax.rem(slot + e, rounds) * each, each)], axis=0)
-            total = total + (pltpu.roll(part, width - e * channels, 1) if e else part)
-        scale = total / (count * (plane * width)) + 1e-06
         for c in range(channels):
-            inverse_ref[d, c] = jnp.broadcast_to((1.0 / scale)[:, c : c + 1], (8, width))
+            total = jnp.zeros((8, width), F32)
+            for q in range(rounds):
+                of_round = functools.reduce(
+                    jnp.add, [wide[(q + e) % rounds, e, c] for e in range(rounds if shared else 1)]
+                )
+                total = jnp.where(slot == q, of_round, total)
+            inverse_ref[d, c] = 1.0 / (total / (count * (plane * width)) + 1e-06)
     for copy in norm_kernel(rounds, tasks, out_ref, inverse_ref, data_refs, buf_ref, kept_ref, sem):
         copy.wait()
 
@@ -469,7 +499,7 @@
     pieces = [(j, n) for j in range(quota) for n in range(CHUNKS)]
     late = pieces[len(pieces) - CHUNKS // HALVES :]
     pieces = pieces[: len(pieces) - len(late)]
-    carried = pieces[len(pieces) * 6 // 7 :]
+    carried = pieces[len(pieces) * 5 // 7 :]
     arrays = []
     tasks = [task(j, n, (j, n) in carried, arrays) for j, n in pieces]
     tile = (rounds, channels, step, width)

time: 44.3 us -> 44.2 us (level)
  transfers between devices with their start and end apart: 8 -> 8, of which waited for: 3 -> 3; matrix products, arithmetic and copies ran while one was open for 0% -> 0% of each run, Pallas kernels for 15% -> 14%
where the time goes in v2:
time: 44.2 us; the launch traced here: 43.9 us
  waiting for transfers between devices  16.6 us (38%)
  starting transfers between devices  14.9 us (34%)
  Pallas kernels  10.1 us (23%)
  local copies, waits for them, and re-layouts  2.2 us (5%)
    ppermute x4, waiting for transfers between devices, send(): lax.ppermute(part, 'round', [(i, (i + d) % rounds) for i in range(rounds)])  9.02 us
    all_to_all x1, waiting for transfers between devices, body(): lax.all_to_all(stat, ('round', 'brick'), split_axis=0, concat_axis=0, til...  7.09 us
    all_to_all x1, starting transfers between devices, body(): lax.all_to_all(stat, ('round', 'brick'), split_axis=0, concat_axis=0, til...  6.39 us
    ppermute x4, starting transfers between devices, send(): lax.ppermute(part, 'round', [(i, (i + d) % rounds) for i in range(rounds)])  5.2 us
    pallas_call x3, Pallas kernels, filtered(): pl.pallas_call(functools.partial(filter_kernel, groups, not sums, len(hal...  4.4 us
    ppermute x3, starting transfers between devices, body(): halo.append(lax.ppermute(swap, 'brick', links))  3.34 us
    unnamed x10, local copies, waits for them, and re-layouts  2.2 us
    pallas_call x1, Pallas kernels, body(): pl.pallas_call(functools.partial(load_kernel, firsts), in_specs=[HBM] * 4...  1.61 us
  transfers between devices with their start and end apart: 8, of which 3 were waited for; matrix products, arithmetic and copies ran while one was open for 0% of the time, Pallas kernels for 14%

profile of v2, /device:TPU:0, one launch (start us, length us, event | category | flops | bytes accessed | tf_op | source)
XLA Modules:
  0.0 43.9 jit_solution(10327955212418040174)
XLA Ops:
  0.0 0.0 copy-start
  0.0 1.6 %load.1 = (bf16[1,4,256,128]{3,2,1,0:T(8,128)(2,1)S(1)}, s32[1,8]{1,0:T(1,128)S(4)}, f32[1,8]{1,0:T(1,128)S(4)}, s32[128]{0:T(128)S(4)}) custom-call(s32[1,8]{1,0:T(1,128)} %shift_hbm.1, f32[1,8]{1,0:T(1,128)} %frac_hbm.1, s32[128]{0:T(128)} %valid_hbm.1, bf16[8,4,256,128]{3,2,1,0:T(8,128)(2,1)} %bitcast.5), custom_call_target="tpu_custom_call" | custom-call | tf_op jit(solution)/shard_map/load/pallas_call | solution.py:406
  1.6 0.2 copy-done
  1.8 0.0 copy-start.1
  1.8 1.0 %copy-done.1 = bf16[1024,256]{1,0:T(8,128)(2,1)S(1)} copy-done((bf16[1024,256]{1,0:T(8,128)(2,1)S(1)}, bf16[1024,256]{1,0:T(8,128)(2,1)}, u32[]{:S(2)}) %copy-start.1) | copy-done | bytes 524312
  2.9 0.0 copy-start.2
  2.9 0.9 %copy-done.2 = f32[2,256,128]{2,1,0:T(8,128)S(1)} copy-done((f32[2,256,128]{2,1,0:T(8,128)S(1)}, f32[2,256,128]{2,1,0:T(8,128)}, u32[]{:S(2)}) %copy-start.2) | copy-done | bytes 262168
  3.8 0.0 copy-start.3
  3.8 1.3 %shard_map.64 = (bf16[2,4,256,128]{3,2,1,0:T(8,128)(2,1)S(1)}, bf16[4,256,128]{2,1,0:T(8,128)(2,1)S(1)}, f32[4,8,128]{2,1,0:T(8,128)S(1)}) custom-call(s32[1,8]{1,0:T(1,128)S(4)} %get-tuple-element.25.shift_ref, f32[1,8]{1,0:T(1,128)S(4)} %get-tuple-element.26.frac_ref, s32[128]{0:T(128)S(4)} %get-tuple-element.27.valid_ref, ...), custom_call_target="tpu_custom_call" | custom-call | tf_op jit(solution)/shard_map/pallas_call | solution.py:431
  5.1 3.0 %collective-permute-start.4 = (bf16[2,4,256,128]{3,2,1,0:T(8,128)(2,1)S(1)}, bf16[2,4,256,128]{3,2,1,0:T(8,128)(2,1)S(1)}, u32[]{:S(2)}, u32[]{:S(2)}) collective-permute-start(bf16[2,4,256,128]{3,2,1,0:T(8,128)(2,1)S(1)} %get-tuple-element.38), channel_id=1, source_target_pairs={{0,16},{16,0},{1,17},{17,1},{2,18},{18,2},{3,19},{19,3},{4,20},{20... | collective-permute-start | bytes 1572872 | tf_op jit(solution)/shard_map/ppermute | solution.py:426
  8.2 0.1 collective-permute-start.3
  8.2 0.2 pack.1
  8.4 0.1 collective-permute-start
  8.5 0.5 %collective-permute-start.2 = (bf16[256,128]{1,0:T(8,128)(2,1)S(1)}, bf16[256,128]{1,0:T(8,128)(2,1)S(1)}, u32[]{:S(2)}, u32[]{:S(2)}) collective-permute-start(bf16[256,128]{1,0:T(8,128)(2,1)S(1)} %get-tuple-element.29), channel_id=1, source_target_pairs={{3,4},{4,3},{7,8},{8,7},{11,12},{12,11},{5,6},{6,5},{9,10},{10,9},... | collective-permute-start | bytes 196616 | tf_op jit(solution)/shard_map/ppermute | solution.py:454
  9.0 2.8 %collective-permute-start.1 = (bf16[256,128]{1,0:T(8,128)(2,1)S(1)}, bf16[256,128]{1,0:T(8,128)(2,1)S(1)}, u32[]{:S(2)}, u32[]{:S(2)}) collective-permute-start(bf16[256,128]{1,0:T(8,128)(2,1)S(1)} %get-tuple-element.29), channel_id=1, source_target_pairs={{1,2},{2,1},{5,6},{6,5},{9,10},{10,9},{13,14},{14,13},{0,3},{3,0},... | collective-permute-start | bytes 196616 | tf_op jit(solution)/shard_map/ppermute | solution.py:454
  11.8 0.0 copy-done.3
  11.8 1.7 %shard_map.65 = (bf16[3,4,256,128]{3,2,1,0:T(8,128)(2,1)S(1)}, f32[4,8,128]{2,1,0:T(8,128)S(1)}) custom-call(s32[1,8]{1,0:T(1,128)S(4)} %get-tuple-element.25.shift_ref, f32[1,8]{1,0:T(1,128)S(4)} %get-tuple-element.26.frac_ref, s32[128]{0:T(128)S(4)} %get-tuple-element.27.valid_ref, bf16[8,4,256,128]{3,2,1,0:T(8,128)(2,1)S(1)} %bitcast.8, ...), custom_call_target="tpu_custom_call" | custom-call | tf_op jit(solution)/shard_map/pallas_call | solution.py:431
  13.5 0.0 collective-permute-done.refs_0_
  13.5 0.0 collective-permute-done.2.refs_2_
  13.5 0.5 %collective-permute-done.1.refs_1_ = bf16[256,128]{1,0:T(8,128)(2,1)S(1)} collective-permute-done((bf16[256,128]{1,0:T(8,128)(2,1)S(1)}, bf16[256,128]{1,0:T(8,128)(2,1)S(1)}, u32[]{:S(2)}, u32[]{:S(2)}) %collective-permute-start.1) | collective-permute-done | bytes 65568 | tf_op jit(solution)/shard_map/ppermute | solution.py:454
  14.0 0.0 copy-start.4
  14.0 1.4 %shard_map.66 = (bf16[1,4,256,128]{3,2,1,0:T(8,128)(2,1)S(1)}, bf16[1,4,128,128]{3,2,1,0:T(8,128)(2,1)S(1)}, bf16[1,4,128,128]{3,2,1,0:T(8,128)(2,1)S(1)}, f32[4,8,128]{2,1,0:T(8,128)S(1)}) custom-call(s32[1,8]{1,0:T(1,128)S(4)} %get-tuple-element.25.shift_ref, f32[1,8]{1,0:T(1,128)S(4)} %get-tuple-element.26.frac_ref, s32[128]{0:T(128)S(4)} %get-tuple-element.27.valid_ref, ...), custom_call_target="tpu_custom_call" | custom-call | tf_op jit(solution)/shard_map/pallas_call | solution.py:431
  15.4 1.7 %collective-permute-start.5 = (bf16[1,4,128,128]{3,2,1,0:T(8,128)(2,1)S(1)}, bf16[1,4,128,128]{3,2,1,0:T(8,128)(2,1)S(1)}, u32[]{:S(2)}, u32[]{:S(2)}) collective-permute-start(bf16[1,4,128,128]{3,2,1,0:T(8,128)(2,1)S(1)} %get-tuple-element.40), channel_id=1, source_target_pairs={{0,16},{16,0},{1,17},{17,1},{2,18},{18,2},{3,19},{19,3},{4,20},{20... | collective-permute-start | bytes 393224 | tf_op jit(solution)/shard_map/ppermute | solution.py:426
  17.2 0.4 collective-permute-start.6
  17.5 9.0 %collective-permute-done.3.refs_0_ = bf16[1,4,256,128]{3,2,1,0:T(8,128)(2,1)S(1)} collective-permute-done((bf16[1,4,256,128]{3,2,1,0:T(8,128)(2,1)S(1)}, bf16[1,4,256,128]{3,2,1,0:T(8,128)(2,1)S(1)}, u32[]{:S(2)}, u32[]{:S(2)}) %collective-permute-start.3) | collective-permute-done | bytes 262176 | tf_op jit(solution)/shard_map/ppermute | solution.py:426
  26.5 1.4 %k4.1 = (bf16[1,4,256,128]{3,2,1,0:T(8,128)(2,1)S(1)}, f32[32,1,128]{2,1,0:T(1,128)}) custom-call(s32[1,8]{1,0:T(1,128)S(4)} %get-tuple-element.25.shift_ref, f32[1,8]{1,0:T(1,128)S(4)} %get-tuple-element.26.frac_ref, s32[128]{0:T(128)S(4)} %get-tuple-element.27.valid_ref, bf16[1024,256]{1,0:T(8,128)(2,1)S(1)} %copy-done.1, f32[2,256,128]{2,1,0:T(8,128)S(1)} %copy-done.3, ...), custom_call_target="tpu_custom_call" | custom-call | tf_op jit(solution)/shard_map/k4/pallas_call | solution.py:469
  27.9 6.4 %all-to-all-start = ((f32[32,1,128]{2,1,0:T(1,128)}), f32[32,1,128]{2,1,0:T(1,128)S(1)}, u32[]{:S(2)}, u32[]{:S(2)}) async-start(f32[32,1,128]{2,1,0:T(1,128)} %get-tuple-element.35), calls=%async_computation | async-start | bytes 32768 | tf_op jit(solution)/shard_map/all_to_all | solution.py:478
  34.3 0.0 collective-permute-done.5.refs_4_
  34.3 7.1 %all-to-all-done.stat_ref = f32[32,1,128]{2,1,0:T(1,128)S(1)} async-done(((f32[32,1,128]{2,1,0:T(1,128)}), f32[32,1,128]{2,1,0:T(1,128)S(1)}, u32[]{:S(2)}, u32[]{:S(2)}) %all-to-all-start) | async-done | bytes 16416 | tf_op jit(solution)/shard_map/all_to_all | solution.py:478
  41.4 0.0 collective-permute-done.4.refs_2_
  41.4 0.0 copy-done.4
  41.4 1.5 %norm1.1 = (bf16[2,1,4,4,256,128]{5,4,3,2,1,0:T(8,128)(2,1)}, f32[2,4,8,128]{3,2,1,0:T(8,128)S(1)}, bf16[4,2,4,64,128]{4,3,2,1,0:T(8,128)(2,1)S(1)}) custom-call(s32[1,128]{1,0:T(1,128)S(1)} %bitcast.10, f32[32,1,128]{2,1,0:T(1,128)S(1)} %all-to-all-done.stat_ref, bf16[3,4,256,128]{3,2,1,0:T(8,128)(2,1)S(1)} %get-tuple-element.36.refs_0_, ...), custom_call_target="tpu_custom_call" | custom-call | tf_op jit(solution)/shard_map/norm1/pallas_call | solution.py:508
  42.9 0.0 collective-permute-done.6.refs_1_
  42.9 1.0 %norm2.1 = bf16[2,1,4,4,256,128]{5,4,3,2,1,0:T(8,128)(2,1)} custom-call(bf16[2,1,4,4,256,128]{5,4,3,2,1,0:T(8,128)(2,1)} %get-tuple-element.41.result_ref, f32[2,4,8,128]{3,2,1,0:T(8,128)S(1)} %get-tuple-element.42.inverse_ref, bf16[4,2,4,64,128]{4,3,2,1,0:T(8,128)(2,1)S(1)} %get-tuple-element.43.kept_ref, ...), custom_call_target="tpu_custom_call", output_to_operand_aliasing={{}: (0, {})} | custom-call | tf_op jit(solution)/shard_map/norm2/pallas_call | solution.py:524
Async XLA Ops:
  0.0 1.8 %copy-start = (bf16[1,8,4,32,8,128]{5,4,3,2,1,0:T(8,128)(2,1)S(1)}, bf16[1,8,4,32,8,128]{5,4,3,2,1,0:T(8,128)(2,1)}, u32[]{:S(2)}) copy-start(bf16[1,8,4,32,8,128]{5,4,3,2,1,0:T(8,128)(2,1)} %param.6) | copy-start | bytes 6291460
  1.8 1.0 %copy-start.1 = (bf16[1024,256]{1,0:T(8,128)(2,1)S(1)}, bf16[1024,256]{1,0:T(8,128)(2,1)}, u32[]{:S(2)}) copy-start(bf16[1024,256]{1,0:T(8,128)(2,1)} %constant.4.clone.plane_ref) | copy-start | bytes 1572868
  2.9 0.9 %copy-start.2 = (f32[2,256,128]{2,1,0:T(8,128)S(1)}, f32[2,256,128]{2,1,0:T(8,128)}, u32[]{:S(2)}) copy-start(f32[2,256,128]{2,1,0:T(8,128)} %constant.5.clone.line_ref) | copy-start | bytes 786436
  3.8 8.0 %copy-start.3 = (f32[2,256,128]{2,1,0:T(8,128)S(1)}, f32[2,256,128]{2,1,0:T(8,128)}, u32[]{:S(2)}) copy-start(f32[2,256,128]{2,1,0:T(8,128)} %constant.5.clone.line_ref) | copy-start | bytes 786436
  5.1 36.3 %collective-permute-start.4 = (bf16[2,4,256,128]{3,2,1,0:T(8,128)(2,1)S(1)}, bf16[2,4,256,128]{3,2,1,0:T(8,128)(2,1)S(1)}, u32[]{:S(2)}, u32[]{:S(2)}) collective-permute-start(bf16[2,4,256,128]{3,2,1,0:T(8,128)(2,1)S(1)} %get-tuple-element.38), channel_id=1, source_target_pairs={{0,16},{16,0},{1,17},{17,1},{2,18},{18,2},{3,19},{19,3},{4,20},{20... | collective-permute-start | bytes 1572872 | tf_op jit(solution)/shard_map/ppermute | solution.py:426
  8.2 18.4 %collective-permute-start.3 = (bf16[1,4,256,128]{3,2,1,0:T(8,128)(2,1)S(1)}, bf16[1,4,256,128]{3,2,1,0:T(8,128)(2,1)S(1)}, u32[]{:S(2)}, u32[]{:S(2)}) collective-permute-start(bf16[1,4,256,128]{3,2,1,0:T(8,128)(2,1)S(1)} %get-tuple-element.34), channel_id=1, source_target_pairs={{0,16},{16,0},{1,17},{17,1},{2,18},{18,2},{3,19},{19,3},{4,20},{20... | collective-permute-start | bytes 786440 | tf_op jit(solution)/shard_map/ppermute | solution.py:426
  8.4 5.0 %collective-permute-start = (bf16[256,128]{1,0:T(8,128)(2,1)S(1)}, bf16[256,128]{1,0:T(8,128)(2,1)S(1)}, u32[]{:S(2)}, u32[]{:S(2)}) collective-permute-start(bf16[256,128]{1,0:T(8,128)(2,1)S(1)} %get-tuple-element.28), channel_id=1, source_target_pairs={{0,1},{1,0},{2,3},{3,2},{4,5},{5,4},{6,7},{7,6},{8,9},{9,8},{10,11... | collective-permute-start | bytes 196616 | tf_op jit(solution)/shard_map/ppermute | solution.py:454
  8.5 5.0 %collective-permute-start.2 = (bf16[256,128]{1,0:T(8,128)(2,1)S(1)}, bf16[256,128]{1,0:T(8,128)(2,1)S(1)}, u32[]{:S(2)}, u32[]{:S(2)}) collective-permute-start(bf16[256,128]{1,0:T(8,128)(2,1)S(1)} %get-tuple-element.29), channel_id=1, source_target_pairs={{3,4},{4,3},{7,8},{8,7},{11,12},{12,11},{5,6},{6,5},{9,10},{10,9},... | collective-permute-start | bytes 196616 | tf_op jit(solution)/shard_map/ppermute | solution.py:454
  9.0 5.0 %collective-permute-start.1 = (bf16[256,128]{1,0:T(8,128)(2,1)S(1)}, bf16[256,128]{1,0:T(8,128)(2,1)S(1)}, u32[]{:S(2)}, u32[]{:S(2)}) collective-permute-start(bf16[256,128]{1,0:T(8,128)(2,1)S(1)} %get-tuple-element.29), channel_id=1, source_target_pairs={{1,2},{2,1},{5,6},{6,5},{9,10},{10,9},{13,14},{14,13},{0,3},{3,0},... | collective-permute-start | bytes 196616 | tf_op jit(solution)/shard_map/ppermute | solution.py:454
  14.0 27.4 %copy-start.4 = (s32[128]{0:T(128)S(1)}, s32[128]{0:T(128)}, u32[]{:S(2)}) copy-start(s32[128]{0:T(128)} %valid_hbm.1) | copy-start | bytes 1540
  15.4 18.9 %collective-permute-start.5 = (bf16[1,4,128,128]{3,2,1,0:T(8,128)(2,1)S(1)}, bf16[1,4,128,128]{3,2,1,0:T(8,128)(2,1)S(1)}, u32[]{:S(2)}, u32[]{:S(2)}) collective-permute-start(bf16[1,4,128,128]{3,2,1,0:T(8,128)(2,1)S(1)} %get-tuple-element.40), channel_id=1, source_target_pairs={{0,16},{16,0},{1,17},{17,1},{2,18},{18,2},{3,19},{19,3},{4,20},{20... | collective-permute-start | bytes 393224 | tf_op jit(solution)/shard_map/ppermute | solution.py:426
  17.2 25.7 %collective-permute-start.6 = (bf16[1,4,128,128]{3,2,1,0:T(8,128)(2,1)S(1)}, bf16[1,4,128,128]{3,2,1,0:T(8,128)(2,1)S(1)}, u32[]{:S(2)}, u32[]{:S(2)}) collective-permute-start(bf16[1,4,128,128]{3,2,1,0:T(8,128)(2,1)S(1)} %get-tuple-element.44), channel_id=1, source_target_pairs={{0,16},{16,0},{1,17},{17,1},{2,18},{18,2},{3,19},{19,3},{4,20},{20... | collective-permute-start | bytes 393224 | tf_op jit(solution)/shard_map/ppermute | solution.py:426
  27.9 13.5 %all-to-all-start = ((f32[32,1,128]{2,1,0:T(1,128)}), f32[32,1,128]{2,1,0:T(1,128)S(1)}, u32[]{:S(2)}, u32[]{:S(2)}) async-start(f32[32,1,128]{2,1,0:T(1,128)} %get-tuple-element.35), calls=%async_computation | async-start | bytes 32768 | tf_op jit(solution)/shard_map/all_to_all | solution.py:478

commit v3 on v1

--- a/solution.py
+++ b/solution.py
@@ -311,15 +311,23 @@
     rank = lax.axis_index("round")
     count = jnp.maximum(jnp.sum(valid_ref[...]).astype(F32), 1.0)
     each = stat_ref.shape[0] // rounds
+    sums = [jnp.sum(stat_ref[q * each : (q + 1) * each], axis=0) for q in range(rounds)]
+    wide = {
+        (q, e, c): jnp.broadcast_to(sums[q][:, e * channels + c : e * channels + c + 1], (8, width))
+        for q in range(rounds)
+        for e in range(rounds if shared else 1)
+        for c in range(channels)
+    }
     for d in range(rounds):
         slot = lax.rem(rank + rounds - d, rounds)
-        total = jnp.zeros(stat_ref.shape[1:], F32)
-        for e in range(rounds if shared else 1):
-            part = jnp.sum(stat_ref[pl.ds(lax.rem(slot + e, rounds) * each, each)], axis=0)
-            total = total + (pltpu.roll(part, width - e * channels, 1) if e else part)
-        scale = total / (count * (plane * width)) + 1e-06
         for c in range(channels):
-            inverse_ref[d, c] = jnp.broadcast_to((1.0 / scale)[:, c : c + 1], (8, width))
+            total = jnp.zeros((8, width), F32)
+            for q in range(rounds):
+                of_round = functools.reduce(
+                    jnp.add, [wide[(q + e) % rounds, e, c] for e in range(rounds if shared else 1)]
+                )
+                total = jnp.where(slot == q, of_round, total)
+            inverse_ref[d, c] = 1.0 / (total / (count * (plane * width)) + 1e-06)
     for copy in norm_kernel(rounds, tasks, out_ref, inverse_ref, data_refs, buf_ref, kept_ref, sem):
         copy.wait()
 
@@ -469,7 +477,7 @@
     pieces = [(j, n) for j in range(quota) for n in range(CHUNKS)]
     late = pieces[len(pieces) - CHUNKS // HALVES :]
     pieces = pieces[: len(pieces) - len(late)]
-    carried = pieces[len(pieces) * 6 // 7 :]
+    carried = pieces[len(pieces) * 5 // 7 :]
     arrays = []
     tasks = [task(j, n, (j, n) in carried, arrays) for j, n in pieces]
     tile = (rounds, channels, step, width)

time: 44.3 us -> 44.2 us (level)
  transfers between devices with their start and end apart: 8 -> 8, of which waited for: 3 -> 3; matrix products, arithmetic and copies ran while one was open for 0% -> 0% of each run, Pallas kernels for 15% -> 14%
where the time goes in v3:
time: 44.2 us; the launch traced here: 43.9 us
  waiting for transfers between devices  16.6 us (38%)
  starting transfers between devices  14.9 us (34%)
  Pallas kernels  10.1 us (23%)
  local copies, waits for them, and re-layouts  2.17 us (5%)
    ppermute x4, waiting for transfers between devices, send(): lax.ppermute(part, 'round', [(i, (i + d) % rounds) for i in range(rounds)])  9.02 us
    all_to_all x1, waiting for transfers between devices, body(): lax.all_to_all(stat, ('round', 'brick'), split_axis=0, concat_axis=0, til...  7.09 us
    all_to_all x1, starting transfers between devices, body(): lax.all_to_all(stat, ('round', 'brick'), split_axis=0, concat_axis=0, til...  6.39 us
    ppermute x4, starting transfers between devices, send(): lax.ppermute(part, 'round', [(i, (i + d) % rounds) for i in range(rounds)])  5.2 us
    pallas_call x3, Pallas kernels, filtered(): pl.pallas_call(functools.partial(filter_kernel, groups, not sums, len(hal...  4.4 us
    ppermute x3, starting transfers between devices, body(): halo.append(lax.ppermute(swap, 'brick', links))  3.34 us
    unnamed x10, local copies, waits for them, and re-layouts  2.17 us
    pallas_call x1, Pallas kernels, body(): pl.pallas_call(functools.partial(load_kernel, firsts), in_specs=[HBM] * 4...  1.65 us
  transfers between devices with their start and end apart: 8, of which 3 were waited for; matrix products, arithmetic and copies ran while one was open for 0% of the time, Pallas kernels for 14%

profile of v3, /device:TPU:0, one launch (start us, length us, event | category | flops | bytes accessed | tf_op | source)
XLA Modules:
  0.0 43.9 jit_solution(17935589682403725708)
XLA Ops:
  0.0 0.0 copy-start
  0.0 1.6 %load.1 = (bf16[1,4,256,128]{3,2,1,0:T(8,128)(2,1)S(1)}, s32[1,8]{1,0:T(1,128)S(4)}, f32[1,8]{1,0:T(1,128)S(4)}, s32[128]{0:T(128)S(4)}) custom-call(s32[1,8]{1,0:T(1,128)} %shift_hbm.1, f32[1,8]{1,0:T(1,128)} %frac_hbm.1, s32[128]{0:T(128)} %valid_hbm.1, bf16[8,4,256,128]{3,2,1,0:T(8,128)(2,1)} %bitcast.5), custom_call_target="tpu_custom_call" | custom-call | tf_op jit(solution)/shard_map/load/pallas_call | solution.py:384
  1.7 0.2 copy-done
  1.8 0.0 copy-start.1
  1.8 1.0 %copy-done.1 = bf16[1024,256]{1,0:T(8,128)(2,1)S(1)} copy-done((bf16[1024,256]{1,0:T(8,128)(2,1)S(1)}, bf16[1024,256]{1,0:T(8,128)(2,1)}, u32[]{:S(2)}) %copy-start.1) | copy-done | bytes 524312
  2.9 0.0 copy-start.2
  2.9 0.9 %copy-done.2 = f32[2,256,128]{2,1,0:T(8,128)S(1)} copy-done((f32[2,256,128]{2,1,0:T(8,128)S(1)}, f32[2,256,128]{2,1,0:T(8,128)}, u32[]{:S(2)}) %copy-start.2) | copy-done | bytes 262168
  3.8 0.0 copy-start.3
  3.8 1.3 %shard_map.64 = (bf16[2,4,256,128]{3,2,1,0:T(8,128)(2,1)S(1)}, bf16[4,256,128]{2,1,0:T(8,128)(2,1)S(1)}, f32[4,8,128]{2,1,0:T(8,128)S(1)}) custom-call(s32[1,8]{1,0:T(1,128)S(4)} %get-tuple-element.25.shift_ref, f32[1,8]{1,0:T(1,128)S(4)} %get-tuple-element.26.frac_ref, s32[128]{0:T(128)S(4)} %get-tuple-element.27.valid_ref, ...), custom_call_target="tpu_custom_call" | custom-call | tf_op jit(solution)/shard_map/pallas_call | solution.py:409
  5.1 3.0 %collective-permute-start.4 = (bf16[2,4,256,128]{3,2,1,0:T(8,128)(2,1)S(1)}, bf16[2,4,256,128]{3,2,1,0:T(8,128)(2,1)S(1)}, u32[]{:S(2)}, u32[]{:S(2)}) collective-permute-start(bf16[2,4,256,128]{3,2,1,0:T(8,128)(2,1)S(1)} %get-tuple-element.38), channel_id=1, source_target_pairs={{0,16},{16,0},{1,17},{17,1},{2,18},{18,2},{3,19},{19,3},{4,20},{20... | collective-permute-start | bytes 1572872 | tf_op jit(solution)/shard_map/ppermute | solution.py:404
  8.2 0.1 collective-permute-start.3
  8.2 0.2 pack.1
  8.4 0.1 collective-permute-start
  8.5 0.5 %collective-permute-start.2 = (bf16[256,128]{1,0:T(8,128)(2,1)S(1)}, bf16[256,128]{1,0:T(8,128)(2,1)S(1)}, u32[]{:S(2)}, u32[]{:S(2)}) collective-permute-start(bf16[256,128]{1,0:T(8,128)(2,1)S(1)} %get-tuple-element.29), channel_id=1, source_target_pairs={{3,4},{4,3},{7,8},{8,7},{11,12},{12,11},{5,6},{6,5},{9,10},{10,9},... | collective-permute-start | bytes 196616 | tf_op jit(solution)/shard_map/ppermute | solution.py:432
  9.0 2.8 %collective-permute-start.1 = (bf16[256,128]{1,0:T(8,128)(2,1)S(1)}, bf16[256,128]{1,0:T(8,128)(2,1)S(1)}, u32[]{:S(2)}, u32[]{:S(2)}) collective-permute-start(bf16[256,128]{1,0:T(8,128)(2,1)S(1)} %get-tuple-element.29), channel_id=1, source_target_pairs={{1,2},{2,1},{5,6},{6,5},{9,10},{10,9},{13,14},{14,13},{0,3},{3,0},... | collective-permute-start | bytes 196616 | tf_op jit(solution)/shard_map/ppermute | solution.py:432
  11.8 0.0 copy-done.3
  11.8 1.7 %shard_map.65 = (bf16[3,4,256,128]{3,2,1,0:T(8,128)(2,1)S(1)}, f32[4,8,128]{2,1,0:T(8,128)S(1)}) custom-call(s32[1,8]{1,0:T(1,128)S(4)} %get-tuple-element.25.shift_ref, f32[1,8]{1,0:T(1,128)S(4)} %get-tuple-element.26.frac_ref, s32[128]{0:T(128)S(4)} %get-tuple-element.27.valid_ref, bf16[8,4,256,128]{3,2,1,0:T(8,128)(2,1)S(1)} %bitcast.8, ...), custom_call_target="tpu_custom_call" | custom-call | tf_op jit(solution)/shard_map/pallas_call | solution.py:409
  13.5 0.0 collective-permute-done.refs_0_
  13.5 0.0 collective-permute-done.2.refs_2_
  13.5 0.5 %collective-permute-done.1.refs_1_ = bf16[256,128]{1,0:T(8,128)(2,1)S(1)} collective-permute-done((bf16[256,128]{1,0:T(8,128)(2,1)S(1)}, bf16[256,128]{1,0:T(8,128)(2,1)S(1)}, u32[]{:S(2)}, u32[]{:S(2)}) %collective-permute-start.1) | collective-permute-done | bytes 65568 | tf_op jit(solution)/shard_map/ppermute | solution.py:432
  14.0 0.0 copy-start.4
  14.0 1.4 %shard_map.66 = (bf16[1,4,256,128]{3,2,1,0:T(8,128)(2,1)S(1)}, bf16[1,4,128,128]{3,2,1,0:T(8,128)(2,1)S(1)}, bf16[1,4,128,128]{3,2,1,0:T(8,128)(2,1)S(1)}, f32[4,8,128]{2,1,0:T(8,128)S(1)}) custom-call(s32[1,8]{1,0:T(1,128)S(4)} %get-tuple-element.25.shift_ref, f32[1,8]{1,0:T(1,128)S(4)} %get-tuple-element.26.frac_ref, s32[128]{0:T(128)S(4)} %get-tuple-element.27.valid_ref, ...), custom_call_target="tpu_custom_call" | custom-call | tf_op jit(solution)/shard_map/pallas_call | solution.py:409
  15.4 1.7 %collective-permute-start.5 = (bf16[1,4,128,128]{3,2,1,0:T(8,128)(2,1)S(1)}, bf16[1,4,128,128]{3,2,1,0:T(8,128)(2,1)S(1)}, u32[]{:S(2)}, u32[]{:S(2)}) collective-permute-start(bf16[1,4,128,128]{3,2,1,0:T(8,128)(2,1)S(1)} %get-tuple-element.40), channel_id=1, source_target_pairs={{0,16},{16,0},{1,17},{17,1},{2,18},{18,2},{3,19},{19,3},{4,20},{20... | collective-permute-start | bytes 393224 | tf_op jit(solution)/shard_map/ppermute | solution.py:404
  17.2 0.4 collective-permute-start.6
  17.5 9.0 %collective-permute-done.3.refs_0_ = bf16[1,4,256,128]{3,2,1,0:T(8,128)(2,1)S(1)} collective-permute-done((bf16[1,4,256,128]{3,2,1,0:T(8,128)(2,1)S(1)}, bf16[1,4,256,128]{3,2,1,0:T(8,128)(2,1)S(1)}, u32[]{:S(2)}, u32[]{:S(2)}) %collective-permute-start.3) | collective-permute-done | bytes 262176 | tf_op jit(solution)/shard_map/ppermute | solution.py:404
  26.5 1.4 %k4.1 = (bf16[1,4,256,128]{3,2,1,0:T(8,128)(2,1)S(1)}, f32[32,1,128]{2,1,0:T(1,128)}) custom-call(s32[1,8]{1,0:T(1,128)S(4)} %get-tuple-element.25.shift_ref, f32[1,8]{1,0:T(1,128)S(4)} %get-tuple-element.26.frac_ref, s32[128]{0:T(128)S(4)} %get-tuple-element.27.valid_ref, bf16[1024,256]{1,0:T(8,128)(2,1)S(1)} %copy-done.1, f32[2,256,128]{2,1,0:T(8,128)S(1)} %copy-done.3, ...), custom_call_target="tpu_custom_call" | custom-call | tf_op jit(solution)/shard_map/k4/pallas_call | solution.py:447
  27.9 6.4 %all-to-all-start = ((f32[32,1,128]{2,1,0:T(1,128)}), f32[32,1,128]{2,1,0:T(1,128)S(1)}, u32[]{:S(2)}, u32[]{:S(2)}) async-start(f32[32,1,128]{2,1,0:T(1,128)} %get-tuple-element.35), calls=%async_computation | async-start | bytes 32768 | tf_op jit(solution)/shard_map/all_to_all | solution.py:456
  34.3 0.0 collective-permute-done.5.refs_4_
  34.3 7.1 %all-to-all-done.stat_ref = f32[32,1,128]{2,1,0:T(1,128)S(1)} async-done(((f32[32,1,128]{2,1,0:T(1,128)}), f32[32,1,128]{2,1,0:T(1,128)S(1)}, u32[]{:S(2)}, u32[]{:S(2)}) %all-to-all-start) | async-done | bytes 16416 | tf_op jit(solution)/shard_map/all_to_all | solution.py:456
  41.4 0.0 collective-permute-done.4.refs_2_
  41.4 0.0 copy-done.4
  41.4 1.5 %norm1.1 = (bf16[2,1,4,4,256,128]{5,4,3,2,1,0:T(8,128)(2,1)}, f32[2,4,8,128]{3,2,1,0:T(8,128)S(1)}, bf16[4,2,4,64,128]{4,3,2,1,0:T(8,128)(2,1)S(1)}) custom-call(s32[1,128]{1,0:T(1,128)S(1)} %bitcast.10, f32[32,1,128]{2,1,0:T(1,128)S(1)} %all-to-all-done.stat_ref, bf16[3,4,256,128]{3,2,1,0:T(8,128)(2,1)S(1)} %get-tuple-element.36.refs_0_, ...), custom_call_target="tpu_custom_call" | custom-call | tf_op jit(solution)/shard_map/norm1/pallas_call | solution.py:486
  42.9 0.0 collective-permute-done.6.refs_1_
  42.9 1.0 %norm2.1 = bf16[2,1,4,4,256,128]{5,4,3,2,1,0:T(8,128)(2,1)} custom-call(bf16[2,1,4,4,256,128]{5,4,3,2,1,0:T(8,128)(2,1)} %get-tuple-element.41.result_ref, f32[2,4,8,128]{3,2,1,0:T(8,128)S(1)} %get-tuple-element.42.inverse_ref, bf16[4,2,4,64,128]{4,3,2,1,0:T(8,128)(2,1)S(1)} %get-tuple-element.43.kept_ref, ...), custom_call_target="tpu_custom_call", output_to_operand_aliasing={{}: (0, {})} | custom-call | tf_op jit(solution)/shard_map/norm2/pallas_call | solution.py:502
Async XLA Ops:
  0.0 1.8 %copy-start = (bf16[1,8,4,32,8,128]{5,4,3,2,1,0:T(8,128)(2,1)S(1)}, bf16[1,8,4,32,8,128]{5,4,3,2,1,0:T(8,128)(2,1)}, u32[]{:S(2)}) copy-start(bf16[1,8,4,32,8,128]{5,4,3,2,1,0:T(8,128)(2,1)} %param.6) | copy-start | bytes 6291460
  1.8 1.0 %copy-start.1 = (bf16[1024,256]{1,0:T(8,128)(2,1)S(1)}, bf16[1024,256]{1,0:T(8,128)(2,1)}, u32[]{:S(2)}) copy-start(bf16[1024,256]{1,0:T(8,128)(2,1)} %constant.4.clone.plane_ref) | copy-start | bytes 1572868
  2.9 0.9 %copy-start.2 = (f32[2,256,128]{2,1,0:T(8,128)S(1)}, f32[2,256,128]{2,1,0:T(8,128)}, u32[]{:S(2)}) copy-start(f32[2,256,128]{2,1,0:T(8,128)} %constant.5.clone.line_ref) | copy-start | bytes 786436
  3.8 8.0 %copy-start.3 = (f32[2,256,128]{2,1,0:T(8,128)S(1)}, f32[2,256,128]{2,1,0:T(8,128)}, u32[]{:S(2)}) copy-start(f32[2,256,128]{2,1,0:T(8,128)} %constant.5.clone.line_ref) | copy-start | bytes 786436
  5.1 36.3 %collective-permute-start.4 = (bf16[2,4,256,128]{3,2,1,0:T(8,128)(2,1)S(1)}, bf16[2,4,256,128]{3,2,1,0:T(8,128)(2,1)S(1)}, u32[]{:S(2)}, u32[]{:S(2)}) collective-permute-start(bf16[2,4,256,128]{3,2,1,0:T(8,128)(2,1)S(1)} %get-tuple-element.38), channel_id=1, source_target_pairs={{0,16},{16,0},{1,17},{17,1},{2,18},{18,2},{3,19},{19,3},{4,20},{20... | collective-permute-start | bytes 1572872 | tf_op jit(solution)/shard_map/ppermute | solution.py:404
  8.2 18.4 %collective-permute-start.3 = (bf16[1,4,256,128]{3,2,1,0:T(8,128)(2,1)S(1)}, bf16[1,4,256,128]{3,2,1,0:T(8,128)(2,1)S(1)}, u32[]{:S(2)}, u32[]{:S(2)}) collective-permute-start(bf16[1,4,256,128]{3,2,1,0:T(8,128)(2,1)S(1)} %get-tuple-element.34), channel_id=1, source_target_pairs={{0,16},{16,0},{1,17},{17,1},{2,18},{18,2},{3,19},{19,3},{4,20},{20... | collective-permute-start | bytes 786440 | tf_op jit(solution)/shard_map/ppermute | solution.py:404
  8.4 5.0 %collective-permute-start = (bf16[256,128]{1,0:T(8,128)(2,1)S(1)}, bf16[256,128]{1,0:T(8,128)(2,1)S(1)}, u32[]{:S(2)}, u32[]{:S(2)}) collective-permute-start(bf16[256,128]{1,0:T(8,128)(2,1)S(1)} %get-tuple-element.28), channel_id=1, source_target_pairs={{0,1},{1,0},{2,3},{3,2},{4,5},{5,4},{6,7},{7,6},{8,9},{9,8},{10,11... | collective-permute-start | bytes 196616 | tf_op jit(solution)/shard_map/ppermute | solution.py:432
  8.5 5.0 %collective-permute-start.2 = (bf16[256,128]{1,0:T(8,128)(2,1)S(1)}, bf16[256,128]{1,0:T(8,128)(2,1)S(1)}, u32[]{:S(2)}, u32[]{:S(2)}) collective-permute-start(bf16[256,128]{1,0:T(8,128)(2,1)S(1)} %get-tuple-element.29), channel_id=1, source_target_pairs={{3,4},{4,3},{7,8},{8,7},{11,12},{12,11},{5,6},{6,5},{9,10},{10,9},... | collective-permute-start | bytes 196616 | tf_op jit(solution)/shard_map/ppermute | solution.py:432
  9.0 5.0 %collective-permute-start.1 = (bf16[256,128]{1,0:T(8,128)(2,1)S(1)}, bf16[256,128]{1,0:T(8,128)(2,1)S(1)}, u32[]{:S(2)}, u32[]{:S(2)}) collective-permute-start(bf16[256,128]{1,0:T(8,128)(2,1)S(1)} %get-tuple-element.29), channel_id=1, source_target_pairs={{1,2},{2,1},{5,6},{6,5},{9,10},{10,9},{13,14},{14,13},{0,3},{3,0},... | collective-permute-start | bytes 196616 | tf_op jit(solution)/shard_map/ppermute | solution.py:432
  14.0 27.4 %copy-start.4 = (s32[128]{0:T(128)S(1)}, s32[128]{0:T(128)}, u32[]{:S(2)}) copy-start(s32[128]{0:T(128)} %valid_hbm.1) | copy-start | bytes 1540
  15.4 18.9 %collective-permute-start.5 = (bf16[1,4,128,128]{3,2,1,0:T(8,128)(2,1)S(1)}, bf16[1,4,128,128]{3,2,1,0:T(8,128)(2,1)S(1)}, u32[]{:S(2)}, u32[]{:S(2)}) collective-permute-start(bf16[1,4,128,128]{3,2,1,0:T(8,128)(2,1)S(1)} %get-tuple-element.40), channel_id=1, source_target_pairs={{0,16},{16,0},{1,17},{17,1},{2,18},{18,2},{3,19},{19,3},{4,20},{20... | collective-permute-start | bytes 393224 | tf_op jit(solution)/shard_map/ppermute | solution.py:404
  17.2 25.7 %collective-permute-start.6 = (bf16[1,4,128,128]{3,2,1,0:T(8,128)(2,1)S(1)}, bf16[1,4,128,128]{3,2,1,0:T(8,128)(2,1)S(1)}, u32[]{:S(2)}, u32[]{:S(2)}) collective-permute-start(bf16[1,4,128,128]{3,2,1,0:T(8,128)(2,1)S(1)} %get-tuple-element.44), channel_id=1, source_target_pairs={{0,16},{16,0},{1,17},{17,1},{2,18},{18,2},{3,19},{19,3},{4,20},{20... | collective-permute-start | bytes 393224 | tf_op jit(solution)/shard_map/ppermute | solution.py:404
  27.9 13.5 %all-to-all-start = ((f32[32,1,128]{2,1,0:T(1,128)}), f32[32,1,128]{2,1,0:T(1,128)S(1)}, u32[]{:S(2)}, u32[]{:S(2)}) async-start(f32[32,1,128]{2,1,0:T(1,128)} %get-tuple-element.35), calls=%async_computation | async-start | bytes 32768 | tf_op jit(solution)/shard_map/all_to_all | solution.py:456
